TPU v7x, 128 devices: a whole 4x4x4 slice. The times are simulated.
128 devices in a mesh: seq: 32 (over x_lo, z, y), head: 4 (over x_hi, core).
Axes of the slice: x: 4 (x_hi: 2, x_lo: 2; x = x_hi * 2 + x_lo), y: 4, z: 4, core: 2. Of those that a mesh axis runs over, the one named last changes fastest.
Arguments:
- queries: bfloat16 [16384, 5120], P('seq', 'head'), may hold values from -6 to 6
- keys: bfloat16 [16384, 5120], P('seq', 'head'), may hold values from -6 to 6
- values: bfloat16 [16384, 5120], P('seq', 'head'), may hold values from -6 to 6
- token_rate: float32 [16384, 8], P('seq', 'head'), may hold values from 0.1 to 1
- head_rate: float32 [8], P('head'), may hold values from 0.2 to 1
- fast_weights: bfloat16 [8, 3, 640, 640], P('head'), may hold values from -0.25 to 0.25
- ttt_gain: float32 [5120], P('head'), may hold values from 0.5 to 1.5
- out_weight: bfloat16 [5120, 5120], P('head', 'seq'), may hold values from -0.078125 to 0.078125
Outputs:
- mixed: bfloat16 [16384, 5120], P('seq', 'head')
All inputs are finite; a program needn't handle non-finite values.
Results may differ from a plain program's by a relative error of at most 0.03.
Values may be sent and summed in bfloat16 or wider, within the bound.
No kernel may reach another device: no remote copies, remote signals or barrier semaphores. Data moves between devices by JAX's collectives and lax.ppermute only.
A program may use at most 128 MiB of HBM per device.

v0:
```python
import functools

import jax
import jax.numpy as jnp
from jax import lax
from jax.experimental import pallas as pl
from jax.experimental.pallas import tpu as pltpu
from jax.sharding import Mesh, PartitionSpec as P


AHD = 128
EPS = 1e-06
f32 = jnp.float32
bf16 = jnp.bfloat16


def hop(block, axis, distance):
    n = lax.axis_size(axis)
    return lax.ppermute(block, axis, [(i, (i + distance) % n) for i in range(n)])


def along_x(block, route):
    place = (0, 2, 1, 3)
    return lax.ppermute(block, ("xl", "xh"), [(place[a], place[b]) for a, b in route])


def next_ring(block, distance):
    axes = ("xl", "z", "y")
    route = [(i, i + 4) for i in range(28) if (i - distance) % 4 >= 2]
    return lax.ppermute(block, axes, route)


def dot(a, b, ca, cb):
    return lax.dot_general(a, b, (((ca,), (cb,)), ((), ())), preferred_element_type=f32)


def descent_kernel(at_ref, k_ref, t_ref, kg_ref, tg_ref, w_ref, out_ref, d_ref):
    first = pl.program_id(0) == 0
    k = jnp.where(first, k_ref[...], kg_ref[...])
    target = jnp.where(first, t_ref[...], tg_ref[...])
    gate = dot(k, w_ref[0, 0], 1, 0)
    up = dot(k, w_ref[0, 1], 1, 0)
    back = dot(target, w_ref[0, 2], 1, 1)
    s = jax.nn.sigmoid(gate)
    silu = gate * s
    act = (silu * up).astype(bf16)
    grad_gate = (back * up * (s * (1.0 + gate * (1.0 - s)))).astype(bf16)
    grad_up = (back * silu).astype(bf16)
    pairs = ((k, grad_gate), (k, grad_up), (act, target))
    for m, (a, b) in enumerate(pairs):
        d_ref[m] = dot(a, b, 0, 0) + jnp.where(first, 0.0, d_ref[m])

    @pl.when(jnp.logical_not(first))
    def _():
        z, y = at_ref[1], at_ref[2]
        part = out_ref.shape[3]
        for i in range(4):
            for j in range(4):
                row = (4 * i + j) * part
                for m in range(3):
                    block = d_ref[m, row : row + part, :].astype(bf16)
                    out_ref[lax.rem(i - z + 4, 4), lax.rem(j - y + 4, 4), m] = block


def descent_of(at, keys, target, k_got, t_got, weights):
    rows, width = target.shape
    whole = lambda shape: pl.BlockSpec(shape, lambda i, at: (0,) * len(shape))
    out = jax.ShapeDtypeStruct((4, 4, 3, width // 16, width), bf16)
    return pl.pallas_call(
        descent_kernel,
        out_shape=out,
        grid_spec=pltpu.PrefetchScalarGridSpec(
            num_scalar_prefetch=1,
            grid=(2,),
            in_specs=[
                pl.BlockSpec((rows, width), lambda i, at: (0, at[0])),
                *[whole((rows, width))] * 3,
                pl.BlockSpec((1, 3, width, width), lambda i, at: (at[0], 0, 0, 0)),
            ],
            out_specs=whole(out.shape),
            scratch_shapes=[pltpu.VMEM((3, width, width), f32)],
        ),
        compiler_params=pltpu.CompilerParams(vmem_limit_bytes=56 << 20),
        cost_estimate=pl.CostEstimate(
            flops=24 * rows * width * width, bytes_accessed=8 << 20, transcendentals=2 * rows * width
        ),
        name="descent",
    )(at, keys, target, k_got, t_got, weights)


def start_of(d):
    return 2 * d + jnp.where(d >= 2, 1, 0)


def pack_kernel(at_ref, *refs):
    ins, outs = refs[:12], refs[12:]
    for k in range(4):
        for i in range(3):
            outs[k][i, 0] = ins[3 * k + i][...]


def pack(at, queries, keys, values):
    rows = queries.shape[0]

    def spec(k):
        return pl.BlockSpec((rows, AHD), lambda s, at: (0, start_of(lax.rem(at[2] + k, 4)) + s))

    out = pl.BlockSpec((3, 1, rows, AHD), lambda s, at: (0, s, 0, 0))
    return pl.pallas_call(
        pack_kernel,
        out_shape=[jax.ShapeDtypeStruct((3, 3, rows, AHD), bf16)] * 4,
        grid_spec=pltpu.PrefetchScalarGridSpec(
            num_scalar_prefetch=1,
            grid=(3,),
            in_specs=[spec(k) for k in range(4) for _ in range(3)],
            out_specs=[out] * 4,
        ),
        cost_estimate=pl.CostEstimate(flops=0, bytes_accessed=10 << 20, transcendentals=0),
        name="pack",
    )(at, *[queries, keys, values] * 4)


def attend_kernel(tile, at_ref, g0, g1, g2, g3, h0, h1, h2, h3, out_ref, q_ref, kv_ref, sems):
    xl, z, y = at_ref[0], at_ref[1], at_ref[2]
    slot, yb = pl.program_id(0), pl.program_id(1)

    def copies(act):
        for k in range(4):
            at = lax.rem(y - k + 4, 4)
            g, h = (g0, g1, g2, g3)[k], (h0, h1, h2, h3)[k]
            act(pltpu.make_async_copy(g.at[0], q_ref.at[at], sems.at[0, k]))
            act(pltpu.make_async_copy(g.at[pl.ds(1, 2)], kv_ref.at[at + 2], sems.at[1, k]))

            @pl.when(at >= 2)
            def _():
                act(pltpu.make_async_copy(h, kv_ref.at[at - 2], sems.at[2, k]))

    @pl.when((slot == 0) & (yb == 0))
    def _():
        copies(lambda c: c.start())
        copies(lambda c: c.wait())

    neg = f32(-1e30)
    first = (xl == 0) & (z == 0)
    bias1 = jnp.where(first & (yb < 1), neg, f32(0))
    bias2 = jnp.where(first & (yb < 2), neg, f32(0))
    scale = f32(1.0) / jnp.sqrt(f32(AHD))
    row = lax.broadcasted_iota(jnp.int32, (tile, tile), 0)
    col = lax.broadcasted_iota(jnp.int32, (tile, tile), 1)
    own = col <= row
    odd = lax.rem(y, 2)
    shared = slot == 2 - 2 * odd

    def step(t, _):
        here, other = pl.ds(pl.multiple_of(t * tile, tile), tile), pl.ds(pl.multiple_of((1 - t) * tile, tile), tile)
        q = q_ref[yb, slot, here, :]

        def score(d, cols):
            return dot(q, kv_ref[yb + 2 - d, 0, slot, cols, :], 1, 1) * scale

        def weigh(p, d, cols):
            return dot(p.astype(bf16), kv_ref[yb + 2 - d, 1, slot, cols, :], 1, 0)

        edge = 2 - 2 * t
        s0 = jnp.where(own, score(0, here), score(2, here) + bias2)
        s1 = score(1, slice(None)) + bias1
        s2 = score(edge, other) + jnp.where(t == 0, bias2, f32(0))
        top = jnp.maximum(jnp.max(s0, axis=1, keepdims=True), jnp.max(s1, axis=1, keepdims=True))
        top = jnp.maximum(top, jnp.max(s2, axis=1, keepdims=True))
        p0, p1, p2 = jnp.exp(s0 - top), jnp.exp(s1 - top), jnp.exp(s2 - top)
        total = sum(jnp.sum(p, axis=1, keepdims=True) for p in (p0, p1, p2))
        out = weigh(jnp.where(own, p0, 0.0), 0, here) + weigh(jnp.where(own, 0.0, p0), 2, here)
        out += weigh(p1, 1, slice(None)) + weigh(p2, edge, other)
        out_ref[0, 0, here, :] = (out / total).astype(bf16)
        return 0

    lax.fori_loop(jnp.where(shared, odd, 0), jnp.where(shared, odd + 1, 2), step, 0)


def attend(at, gs, hs):
    rows = gs[0].shape[2]
    hbm = pl.BlockSpec(memory_space=pl.ANY)
    return pl.pallas_call(
        functools.partial(attend_kernel, rows // 2),
        out_shape=jax.ShapeDtypeStruct((4, 3, rows, AHD), bf16),
        grid_spec=pltpu.PrefetchScalarGridSpec(
            num_scalar_prefetch=1,
            grid=(3, 4),
            in_specs=[hbm] * 8,
            out_specs=pl.BlockSpec((1, 1, rows, AHD), lambda s, b, at: (lax.rem(at[2] - b + 4, 4), s, 0, 0)),
            scratch_shapes=[
                pltpu.VMEM((4, 3, rows, AHD), bf16),
                pltpu.VMEM((6, 2, 3, rows, AHD), bf16),
                pltpu.SemaphoreType.DMA((3, 4)),
            ],
        ),
        compiler_params=pltpu.CompilerParams(vmem_limit_bytes=40 << 20),
        cost_estimate=pl.CostEstimate(
            flops=12 * rows * rows * 10 * AHD, bytes_accessed=12 << 20, transcendentals=2 * rows * rows * 10
        ),
        name="attend",
    )(at, *gs, *hs)


def columns_kernel(at_ref, r0, r1, r2, r3, own_ref, other_ref, all_ref):
    xl, y = at_ref[0], at_ref[2]
    for k, r in enumerate((r0, r1, r2, r3)):
        all_ref[k] = r[...]
    half = r0.shape[1] // 2
    for head, out_ref in ((xl, own_ref), (1 - xl, other_ref)):
        low, high = lax.rem(2 * head - y + 4, 4), lax.rem(2 * head + 1 - y + 4, 4)
        for j in range(2):
            out_ref[:, j * AHD : (j + 1) * AHD] = all_ref[low, j]
            out_ref[:, (j + 3) * AHD : (j + 4) * AHD] = all_ref[high, j + 1]
        out_ref[:half, 2 * AHD : 3 * AHD] = all_ref[low, 2, :half]
        out_ref[half:, 2 * AHD : 3 * AHD] = all_ref[high, 0, half:]


def columns_of(at, backs):
    rows = backs[0].shape[1]
    vmem = pl.BlockSpec(memory_space=pltpu.VMEM)
    return pl.pallas_call(
        columns_kernel,
        out_shape=[jax.ShapeDtypeStruct((rows, 5 * AHD), bf16)] * 2,
        in_specs=[pl.BlockSpec(memory_space=pltpu.SMEM), *[vmem] * 4],
        out_specs=[vmem] * 2,
        scratch_shapes=[pltpu.VMEM((4, *backs[0].shape), bf16)],
        cost_estimate=pl.CostEstimate(flops=0, bytes_accessed=3 << 20, transcendentals=0),
        name="columns",
    )(at, *backs)


def mean_of(x, axis):
    return jnp.sum(x, axis=axis, keepdims=True) / f32(x.shape[0] if axis == 0 else x.size)


def answer(q, u, gain):
    gate = dot(q, u[0], 1, 0)
    up = dot(q, u[1], 1, 0)
    act = (gate * jax.nn.sigmoid(gate) * up).astype(bf16)
    fast = dot(act, u[2], 1, 0)
    mean = jnp.sum(fast * fast, axis=1, keepdims=True) / f32(fast.shape[1])
    return fast * lax.rsqrt(mean + EPS) * gain


def update_kernel(at_ref, rate_ref, g0, g1, g2, g3, w_ref, q_ref, gain_ref, u_ref, out_ref, d_ref):
    head, z, y = at_ref[0], at_ref[1], at_ref[2]
    part = g0.shape[2]
    for i in range(4):
        for j in range(4):
            row = pl.multiple_of((4 * lax.rem(z + i, 4) + lax.rem(y + j, 4)) * part, 8)
            for m in range(3):
                d_ref[m, pl.ds(row, part), :] = (g0, g1, g2, g3)[i][j, m].astype(f32)
    for m in range(3):
        d = d_ref[m]
        w = w_ref[0, m].astype(f32)
        ww = w * w
        col_w = mean_of(ww, 0)
        mean_w = jnp.sum(col_w, axis=1, keepdims=True) / f32(w.shape[1])
        mean_d = jnp.sum(mean_of(d * d, 0), axis=1, keepdims=True) / f32(w.shape[1])
        factor = rate_ref[head] * jnp.sqrt((mean_w + EPS) / (mean_d + EPS))
        moved = w + factor * d
        col_m = mean_of(moved * moved, 0)
        u_ref[m] = (moved * jnp.sqrt((col_w + EPS) / (col_m + EPS))).astype(bf16)
    out_ref[...] = answer(q_ref[...], u_ref, gain_ref[...])


def update_of(at, rate, sums, weights, q, gain):
    rows, width = q.shape
    whole = lambda shape: pl.BlockSpec(shape, lambda i, at, r: (0,) * len(shape))
    shapes = [jax.ShapeDtypeStruct((3, width, width), bf16), jax.ShapeDtypeStruct((rows, width), f32)]
    return pl.pallas_call(
        update_kernel,
        out_shape=shapes,
        grid_spec=pltpu.PrefetchScalarGridSpec(
            num_scalar_prefetch=2,
            grid=(1,),
            in_specs=[
                *[whole(sums[0].shape)] * 4,
                pl.BlockSpec((1, 3, width, width), lambda i, at, r: (at[0], 0, 0, 0)),
                whole(q.shape),
                pl.BlockSpec((1, width), lambda i, at, r: (0, at[0])),
            ],
            out_specs=[whole(s.shape) for s in shapes],
            scratch_shapes=[pltpu.VMEM((3, width, width), f32)],
        ),
        compiler_params=pltpu.CompilerParams(vmem_limit_bytes=56 << 20),
        cost_estimate=pl.CostEstimate(
            flops=6 * rows * width * width, bytes_accessed=8 << 20, transcendentals=rows * width
        ),
        name="update",
    )(at, rate, *sums, weights, q, gain)


def own_kernel(at_ref, u_ref, q_ref, gain_ref, attn_ref, out_ref):
    out_ref[...] = (answer(q_ref[...], u_ref, gain_ref[...]) + attn_ref[...].astype(f32)).astype(bf16)


def own_of(at, u, queries, gain, attn):
    rows, width = attn.shape
    return pl.pallas_call(
        own_kernel,
        out_shape=jax.ShapeDtypeStruct((rows, width), bf16),
        grid_spec=pltpu.PrefetchScalarGridSpec(
            num_scalar_prefetch=1,
            grid=(1,),
            in_specs=[
                pl.BlockSpec(u.shape, lambda i, at: (0, 0, 0)),
                pl.BlockSpec((rows, width), lambda i, at: (0, at[0])),
                pl.BlockSpec((1, width), lambda i, at: (0, at[0])),
                pl.BlockSpec((rows, width), lambda i, at: (0, 0)),
            ],
            out_specs=pl.BlockSpec((rows, width), lambda i, at: (0, 0)),
        ),
        compiler_params=pltpu.CompilerParams(vmem_limit_bytes=56 << 20),
        cost_estimate=pl.CostEstimate(
            flops=6 * rows * width * width, bytes_accessed=6 << 20, transcendentals=rows * width
        ),
        name="own",
    )(at, u, queries, gain, attn)


def project_kernel(at_ref, f0, f1, f2, f3, a0, a1, a3, a2a, a2b, b0, b1, b3, b2a, b2b, out_ref, w_ref, f_ref, sem):
    z, y, core, x = at_ref[0], at_ref[1], at_ref[2], at_ref[3]
    width, cut = a0.shape[2], a0.shape[3]
    full = cut + b0.shape[3]

    def copy(src, half, g, zb, yb):
        c0 = g * full + half * cut
        row = pl.multiple_of((4 * lax.rem(zb, 2) + yb) * width, 16)
        dst = w_ref.at[pl.ds(row, width), c0 : c0 + src.shape[1]]
        return pltpu.make_async_copy(src, dst, sem.at[half, g, lax.rem(zb, 2), yb])

    for i in range(4):
        for j in range(4):
            for half, (big, small) in enumerate(((z, y), (y, z))):
                far = (a2a, b2a) if j < 2 else (a2b, b2b)
                srcs = ((a0, a1, far[0], a3), (b0, b1, far[1], b3))[half]
                p, q = lax.rem(big + i, 4), lax.rem(small + j, 4)
                zb, yb = (p, q) if half == 0 else (q, p)

                @pl.when(zb // 2 == core)
                def _():
                    for g in range(2):
                        copy(srcs[i].at[j - 2 if i == 2 and j >= 2 else j, g], half, g, zb, yb).start()

    for r, f in enumerate((f0, f1, f2, f3)):
        cols = pl.multiple_of(lax.rem(x + r, 4) * f.shape[1], AHD)
        f_ref[:, pl.ds(cols, f.shape[1])] = f[...]

    def arrive(zb):
        for half, src in enumerate((a0, b0)):
            for g in range(2):
                for yb in range(4):
                    copy(src.at[0, 0], half, g, zb, yb).wait()

    def tile(t, _):
        @pl.when(t == 0)
        def _():
            arrive(0)

        @pl.when(t == 2)
        def _():
            arrive(1)

        cols = pl.ds(pl.multiple_of(t * 2 * AHD, 2 * AHD), 2 * AHD)
        out_ref[:, cols] = dot(f_ref[...], w_ref[cols, :], 1, 1).astype(bf16)
        return 0

    lax.fori_loop(0, out_ref.shape[1] // (2 * AHD), tile, 0)


def project(at, fs, pieces):
    rows, full = fs[0].shape[0], 4 * fs[0].shape[1]
    width = pieces[0].shape[2]
    vmem = pl.BlockSpec(memory_space=pltpu.VMEM)
    hbm = pl.BlockSpec(memory_space=pl.ANY)
    return pl.pallas_call(
        project_kernel,
        out_shape=jax.ShapeDtypeStruct((rows, 8 * width), bf16),
        in_specs=[pl.BlockSpec(memory_space=pltpu.SMEM), *[vmem] * 4, *[hbm] * 10],
        out_specs=vmem,
        scratch_shapes=[
            pltpu.VMEM((8 * width, full), bf16),
            pltpu.VMEM((rows, full), bf16),
            pltpu.SemaphoreType.DMA((2, 2, 2, 4)),
        ],
        compiler_params=pltpu.CompilerParams(vmem_limit_bytes=40 << 20),
        cost_estimate=pl.CostEstimate(
            flops=2 * rows * full * 8 * width, bytes_accessed=10 << 20, transcendentals=0
        ),
        name="project",
    )(at, *fs, *pieces)


def scatter(chunks, axis):
    total = chunks[0].astype(f32)
    got = [hop(chunks[k], axis, k) for k in (1, 3, 2)]
    for g in got:
        total = total + g.astype(f32)
    return total.astype(bf16)


def gather(block, axis):
    got = {k: hop(block, axis, -k) for k in (1, 3, 2)}
    return [block, got[1], got[2], got[3]]


def gather_ring(block, axis):
    up, down = hop(block, axis, -1), hop(block, axis, 1)
    return (block, up, down, hop(up[:2], axis, -1), hop(down[2:], axis, 1))


def body(queries, keys, values, token_rate, head_rate, fast_weights, ttt_gain, out_weight):
    xl, z, y = lax.axis_index("xl"), lax.axis_index("z"), lax.axis_index("y")
    xh, core = lax.axis_index("xh"), lax.axis_index("core")
    x = 2 * xh + xl
    width = fast_weights.shape[2]
    at = jnp.stack([xl, z, y, x]).astype(jnp.int32)

    def cols_of(a, head):
        return lax.dynamic_slice_in_dim(a, head * width, width, 1)

    def target_of(head):
        rate = lax.dynamic_slice_in_dim(token_rate, head, 1, 1)
        return (rate * cols_of(values, head).astype(f32)).astype(bf16)

    k_got = hop(cols_of(keys, 1 - xl), "xl", 1)
    t_got = hop(target_of(1 - xl), "xl", 1)

    turned = out_weight.T
    one = along_x(turned, [(2, 0), (0, 1), (1, 2)])
    two = along_x(turned, [(2, 1), (3, 2), (1, 3)])

    packs = pack(at, queries, keys, values)
    gs = [packs[0]] + [hop(packs[k], "y", k) for k in range(1, 4)]
    parts = descent_of(at, keys, target_of(xl), k_got, t_got, fast_weights)

    low = jnp.where(x == 0, turned, jnp.where(x == 3, two, one))
    high = jnp.where(x == 3, turned, jnp.where(x == 0, one, two))
    pair = jnp.stack([low, high])
    block_a = jnp.stack(gather(pair[:, :, :width], "y"))
    block_b = jnp.stack(gather(pair[:, :, width:], "z"))
    queries_far = lax.optimization_barrier((queries, t_got))[0]
    q_got = hop(cols_of(queries_far, 1 - xl), "xl", 1)

    parts = scatter(parts, "z")
    pieces = (*gather_ring(block_a, "z"), *gather_ring(block_b, "y"))

    hs = [next_ring(gs[k][1:], k) for k in range(4)]

    sums = scatter(parts, "y")
    sums = gather(jnp.stack(gather(sums, "y")), "z")

    done = attend(at, gs, hs)
    backs = [done[0]] + [hop(done[k], "y", -k) for k in range(1, 4)]
    attn, other = columns_of(at, backs)
    attn_got = hop(other, "xl", 1)
    gain = ttt_gain[None, :]
    new, fast = update_of(at, head_rate, sums, fast_weights, q_got, gain)
    fast = (fast + attn_got.astype(f32)).astype(bf16)
    next_fast = along_x(fast, [(i, (i + 3) % 4) for i in range(4)])
    last_fast = along_x(fast, [(i, (i + 1) % 4) for i in range(4)])
    mine_fast = own_of(at, new, queries, gain, attn)
    far_fast = hop(mine_fast, "xh", 1)
    fs = (mine_fast, next_fast, far_fast, last_fast)

    def at_of(place):
        return jnp.stack([z, y, place, x]).astype(jnp.int32)

    sent = project(at_of(1 - core), fs, pieces)
    got = hop(sent, "core", 1)
    fs = lax.optimization_barrier((*fs, sent))[:4]
    mine = project(at_of(core), fs, pieces)
    return (mine.astype(f32) + got.astype(f32)).astype(bf16)


def solution(mesh):
    fine = Mesh(mesh.devices.reshape(2, 4, 4, 2, 2), ("xl", "z", "y", "xh", "core"))
    seq, head = ("xl", "z", "y"), ("xh", "core")
    placed = (
        P(seq, head),
        P(seq, head),
        P(seq, head),
        P(seq, head),
        P(head),
        P(head, None, None, None),
        P(head),
        P(head, seq),
    )
    return jax.shard_map(body, mesh=fine, in_specs=placed, out_specs=P(seq, head), check_vma=False)
```

profile of v0, /device:TPU:1, one launch (start us, length us, event | category | flops | bytes accessed | tf_op | source)
XLA Modules:
  0.0 361.9 jit_solution(3248746423434564846)
XLA Ops:
  0.8 2.5 multiply_convert_fusion
  3.3 2.0 collective-permute-start.1
  6.0 13.3 %collective-permute-done.1.tg_ref = bf16[512,640]{1,0:T(8,128)(2,1)S(1)} collective-permute-done((bf16[512,640]{1,0:T(8,128)(2,1)S(1)}, bf16[512,640]{1,0:T(8,128)(2,1)S(1)}, u32[]{:S(2)}, u32[]{:S(2)}) %collective-permute-start.1) | collective-permute-done | bytes 655392 | tf_op jit(solution)/shard_map/ppermute | solution.py:19
  19.3 14.0 %collective-permute-done.kg_ref = bf16[512,640]{1,0:T(8,128)(2,1)S(1)} collective-permute-done((bf16[512,640]{1,0:T(8,128)(2,1)S(1)}, bf16[512,640]{1,0:T(8,128)(2,1)S(1)}, u32[]{:S(2)}, u32[]{:S(2)}) %collective-permute-start) | collective-permute-done | bytes 655392 | tf_op jit(solution)/shard_map/ppermute | solution.py:19
  34.2 12.2 %descent.1 = bf16[4,4,3,40,640]{4,3,2,1,0:T(8,128)(2,1)} custom-call(s32[4]{0:T(128)} %add_add_fusion.1.at_ref, bf16[512,1280]{1,0:T(8,128)(2,1)} %refs_10_.1, bf16[512,640]{1,0:T(8,128)(2,1)} %get-tuple-element.39.t_ref, bf16[512,640]{1,0:T(8,128)(2,1)} %copy-done.22, bf16[512,640]{1,0:T(8,128)(2,1)} %copy-done.21, bf16[2,3,640,640]{3,2,1,0:T(8,128)(2,1)} %w_ref.3), custom_call_target="tpu_custom_call" | custom-call | flops 5033164800 | bytes 8388608 | tf_op jit(solution)/shard_map/descent/pallas_call | solution.py:69
  46.4 1.7 slice_bitcast_fusion.2
  48.0 2.1 collective-permute-start.2
  50.1 2.2 collective-permute-start.3
  52.3 1.4 collective-permute-start.29
  53.8 5.4 %collective-permute-start.30 = (bf16[160,1280]{1,0:T(8,128)(2,1)S(1)}, bf16[160,1280]{1,0:T(8,128)(2,1)}, u32[]{:S(2)}, u32[]{:S(2)}) collective-permute-start(bf16[160,1280]{1,0:T(8,128)(2,1)S(1)} %bitcast.61), channel_id=1, source_target_pairs={{2,0},{0,64},{64,2},{3,1},{1,65},{65,3},{6,4},{4,68},{68,6},{7,5},... | collective-permute-start | bytes 1228808 | tf_op jit(solution)/shard_map/ppermute | solution.py:24
  59.2 6.3 %pack.1 = (bf16[3,3,512,128]{3,2,1,0:T(8,128)(2,1)}, bf16[3,3,512,128]{3,2,1,0:T(8,128)(2,1)}, bf16[3,3,512,128]{3,2,1,0:T(8,128)(2,1)}, bf16[3,3,512,128]{3,2,1,0:T(8,128)(2,1)}) custom-call(s32[4]{0:T(128)} %add_add_fusion.1.at_ref, bf16[512,1280]{1,0:T(8,128)(2,1)} %q_ref.1, bf16[512,1280]{1,0:T(8,128)(2,1)} %refs_10_.1, bf16[512,1280]{1,0:T(8,128)(2,1)} %refs_11_.1, ...), custom_call_target="tpu_custom_call" | custom-call | bytes 10485760 | tf_op jit(solution)/shard_map/pack/pallas_call | solution.py:109
  65.5 1.4 collective-permute-start.15
  66.9 1.3 slice.74
  68.2 2.7 collective-permute-start.16
  70.9 1.1 collective-permute-start.17
  72.7 1.3 collective-permute-start.4
  74.0 1.2 select_bitcast_fusion
  75.3 11.2 %collective-permute-done.4 = bf16[4,3,40,640]{3,2,1,0:T(8,128)(2,1)S(1)} collective-permute-done((bf16[4,3,40,640]{3,2,1,0:T(8,128)(2,1)S(1)}, bf16[4,3,40,640]{3,2,1,0:T(8,128)(2,1)S(1)}, u32[]{:S(2)}, u32[]{:S(2)}) %collective-permute-start.4) | collective-permute-done | bytes 614432 | tf_op jit(solution)/shard_map/ppermute | solution.py:19
  86.4 17.6 %collective-permute-start.31 = (bf16[2,160,640]{2,1,0:T(8,128)(2,1)S(1)}, bf16[2,160,640]{2,1,0:T(8,128)(2,1)S(1)}, u32[]{:S(2)}, u32[]{:S(2)}) collective-permute-start(bf16[2,160,640]{2,1,0:T(8,128)(2,1)S(1)} %get-tuple-element.43), channel_id=1, source_target_pairs={{0,12},{4,0},{8,4},{12,8},{1,13},{5,1},{9,5},{13,9},{2,14},{6,2},{... | collective-permute-start | bytes 1228808 | tf_op jit(solution)/shard_map/ppermute | solution.py:19
  104.0 1.8 fusion.2
  105.9 2.7 collective-permute-start.6
  108.6 10.1 %collective-permute-done.16.g2 = bf16[3,3,512,128]{3,2,1,0:T(8,128)(2,1)S(1)} collective-permute-done((bf16[3,3,512,128]{3,2,1,0:T(8,128)(2,1)}, bf16[3,3,512,128]{3,2,1,0:T(8,128)(2,1)S(1)}, u32[]{:S(2)}, u32[]{:S(2)}) %collective-permute-start.16) | collective-permute-done | bytes 1179680 | tf_op jit(solution)/shard_map/ppermute | solution.py:19
  119.1 2.1 collective-permute-done.17.g3
  122.3 7.7 %collective-permute-done.31 = bf16[2,160,640]{2,1,0:T(8,128)(2,1)S(1)} collective-permute-done((bf16[2,160,640]{2,1,0:T(8,128)(2,1)S(1)}, bf16[2,160,640]{2,1,0:T(8,128)(2,1)S(1)}, u32[]{:S(2)}, u32[]{:S(2)}) %collective-permute-start.31) | collective-permute-done | bytes 409632 | tf_op jit(solution)/shard_map/ppermute | solution.py:19
  130.0 1.4 collective-permute-start.19
  131.4 3.4 collective-permute-start.20
  137.2 8.6 %collective-permute-start.8 = (bf16[3,40,640]{2,1,0:T(8,128)(2,1)S(1)}, bf16[3,40,640]{2,1,0:T(8,128)(2,1)S(1)}, u32[]{:S(2)}, u32[]{:S(2)}) collective-permute-start(bf16[3,40,640]{2,1,0:T(8,128)(2,1)S(1)} %fusion.6), channel_id=1, source_target_pairs={{0,12},{4,0},{8,4},{12,8},{1,13},{5,1},{9,5},{13,9},{2,14},{6,2},{... | collective-permute-start | bytes 460808 | tf_op jit(solution)/shard_map/ppermute | solution.py:19
  146.6 1.0 collective-permute-start.9
  148.5 3.1 collective-permute-start.10
  151.9 1.1 collective-permute-done.9
  153.0 1.7 collective-permute-start.38
  156.5 1.2 collective-permute-start.40
  157.7 2.7 collective-permute-done.20.h2
  160.3 5.8 %collective-permute-start.14 = (bf16[512,640]{1,0:T(8,128)(2,1)S(1)}, bf16[512,640]{1,0:T(8,128)(2,1)S(1)}, u32[]{:S(2)}, u32[]{:S(2)}) collective-permute-start(bf16[512,640]{1,0:T(8,128)(2,1)S(1)} %constant_dynamic-slice_fusion), channel_id=1, source_target_pairs={{0,64},{64,0},{1,65},{65,1},{2,66},{66,2},{3,67},{67,3},{4,68},{68... | collective-permute-start | bytes 1966088 | tf_op jit(solution)/shard_map/ppermute | solution.py:19
  166.2 17.7 %attend.1 = bf16[4,3,512,128]{3,2,1,0:T(8,128)(2,1)S(1)} custom-call(s32[4]{0:T(128)S(1)} %copy-done.8, bf16[3,3,512,128]{3,2,1,0:T(8,128)(2,1)S(1)} %copy-done.7, bf16[3,3,512,128]{3,2,1,0:T(8,128)(2,1)S(1)} %collective-permute-done.15.g1, bf16[3,3,512,128]{3,2,1,0:T(8,128)(2,1)S(1)} %collective-permute-done.16.g2, ...), custom_call_target="tpu_custom_call" | custom-call | flops 4026531840 | bytes 12582912 | tf_op jit(solution)/shard_map/attend/pallas_call | solution.py:183
  184.1 3.2 collective-permute-start.12
  188.2 2.1 collective-permute-start.23
  190.7 4.4 %collective-permute-done.12.g2 = bf16[4,3,40,640]{3,2,1,0:T(8,128)(2,1)S(1)} collective-permute-done((bf16[4,3,40,640]{3,2,1,0:T(8,128)(2,1)}, bf16[4,3,40,640]{3,2,1,0:T(8,128)(2,1)S(1)}, u32[]{:S(2)}, u32[]{:S(2)}) %collective-permute-start.12) | collective-permute-done | bytes 614432 | tf_op jit(solution)/shard_map/ppermute | solution.py:19
  195.9 2.2 collective-permute-start.42
  198.8 27.8 %collective-permute-done.24.r3 = bf16[3,512,128]{2,1,0:T(8,128)(2,1)S(1)} collective-permute-done((bf16[3,512,128]{2,1,0:T(8,128)(2,1)S(1)}, bf16[3,512,128]{2,1,0:T(8,128)(2,1)S(1)}, u32[]{:S(2)}, u32[]{:S(2)}) %collective-permute-start.24) | collective-permute-done | bytes 393248 | tf_op jit(solution)/shard_map/ppermute | solution.py:19
  226.6 39.5 %collective-permute-start.13 = (bf16[4,3,40,640]{3,2,1,0:T(8,128)(2,1)}, bf16[4,3,40,640]{3,2,1,0:T(8,128)(2,1)}, u32[]{:S(2)}, u32[]{:S(2)}) collective-permute-start(bf16[4,3,40,640]{3,2,1,0:T(8,128)(2,1)} %pad_maximum_fusion.2.g0), channel_id=1, source_target_pairs={{0,16},{16,32},{32,48},{48,0},{1,17},{17,33},{33,49},{49,1},{2,18}... | collective-permute-start | bytes 1843208 | tf_op jit(solution)/shard_map/ppermute | solution.py:19
  266.1 2.8 columns.1
  269.7 1.2 slice.105
  270.9 6.9 %collective-permute-done.13.g3 = bf16[4,3,40,640]{3,2,1,0:T(8,128)(2,1)} collective-permute-done((bf16[4,3,40,640]{3,2,1,0:T(8,128)(2,1)}, bf16[4,3,40,640]{3,2,1,0:T(8,128)(2,1)}, u32[]{:S(2)}, u32[]{:S(2)}) %collective-permute-start.13) | collective-permute-done | bytes 614432 | tf_op jit(solution)/shard_map/ppermute | solution.py:19
  277.8 1.5 collective-permute-start.36
  279.3 8.9 %update.1 = (bf16[3,640,640]{2,1,0:T(8,128)(2,1)}, f32[512,640]{1,0:T(8,128)}) custom-call(s32[4]{0:T(128)} %add_add_fusion.1.at_ref, f32[2]{0:T(128)} %rate_ref.1, bf16[4,3,40,640]{3,2,1,0:T(8,128)(2,1)} %pad_maximum_fusion.2.g0, bf16[4,3,40,640]{3,2,1,0:T(8,128)(2,1)} %copy-done.13, bf16[4,3,40,640]{3,2,1,0:T(8,128)(2,1)} %copy-done.14, ...), custom_call_target="tpu_custom_call" | custom-call | flops 1258291200 | bytes 8388608 | tf_op jit(solution)/shard_map/update/pallas_call | solution.py:272
  288.1 5.7 %own.1.f0 = bf16[512,640]{1,0:T(8,128)(2,1)} custom-call(s32[4]{0:T(128)} %add_add_fusion.1.at_ref, bf16[3,640,640]{2,1,0:T(8,128)(2,1)} %get-tuple-element.19.u_ref, bf16[512,1280]{1,0:T(8,128)(2,1)} %q_ref.1, f32[1,1280]{1,0:T(1,128)} %broadcast_in_dim.3.gain_ref, bf16[512,640]{1,0:T(8,128)(2,1)} %get-tuple-element.24.attn_ref), custom_call_target="tpu_custom_call" | custom-call | flops 1258291200 | bytes 6291456 | tf_op jit(solution)/shard_map/own/pallas_call | solution.py:301
  293.9 6.9 %collective-permute-start.27 = (bf16[512,640]{1,0:T(8,128)(2,1)}, bf16[512,640]{1,0:T(8,128)(2,1)S(1)}, u32[]{:S(2)}, u32[]{:S(2)}) collective-permute-start(bf16[512,640]{1,0:T(8,128)(2,1)} %own.1.f0), channel_id=1, source_target_pairs={{0,2},{2,0},{1,3},{3,1},{4,6},{6,4},{5,7},{7,5},{8,10},{10,8},{9,1... | collective-permute-start | bytes 1966088 | tf_op jit(solution)/shard_map/ppermute | solution.py:19
  300.8 2.1 slice.106
  302.9 2.2 slice.107
  305.1 1.0 collective-permute-start.43
  306.1 2.1 slice.108
  310.6 3.2 collective-permute-start.26
  314.7 1.2 collective-permute-done.37.a2b
  316.0 1.0 collective-permute-done.43.b2a
  316.9 4.5 %collective-permute-done.44.b2b = bf16[2,2,160,640]{3,2,1,0:T(8,128)(2,1)} collective-permute-done((bf16[2,2,160,640]{3,2,1,0:T(8,128)(2,1)}, bf16[2,2,160,640]{3,2,1,0:T(8,128)(2,1)}, u32[]{:S(2)}, u32[]{:S(2)}) %collective-permute-start.44) | collective-permute-done | bytes 819232 | tf_op jit(solution)/shard_map/ppermute | solution.py:19
  321.4 4.3 %collective-permute-done.26.f1 = bf16[512,640]{1,0:T(8,128)(2,1)} collective-permute-done((bf16[512,640]{1,0:T(8,128)(2,1)}, bf16[512,640]{1,0:T(8,128)(2,1)}, u32[]{:S(2)}, u32[]{:S(2)}) %collective-permute-start.26) | collective-permute-done | bytes 655392 | tf_op jit(solution)/shard_map/ppermute | solution.py:24
  325.9 1.1 copy-done
  327.0 1.1 copy-done.2
  328.1 1.1 copy-done.5
  329.2 8.7 %project.2 = bf16[512,1280]{1,0:T(8,128)(2,1)S(1)} custom-call(s32[4]{0:T(128)S(1)} %add_add_fusion.2.at_ref, bf16[512,640]{1,0:T(8,128)(2,1)S(1)} %copy-done, bf16[512,640]{1,0:T(8,128)(2,1)} %collective-permute-done.26.f1, bf16[512,640]{1,0:T(8,128)(2,1)S(1)} %copy-done.5, bf16[512,640]{1,0:T(8,128)(2,1)} %collective-permute-done.28.f3, ...), custom_call_target="tpu_custom_call" | custom-call | flops 3355443200 | bytes 10485760 | tf_op jit(solution)/shard_map/project/pallas_call | solution.py:378
  337.9 13.9 %collective-permute-start.45 = (bf16[512,1280]{1,0:T(8,128)(2,1)S(1)}, bf16[512,1280]{1,0:T(8,128)(2,1)S(1)}, u32[]{:S(2)}, u32[]{:S(2)}) collective-permute-start(bf16[512,1280]{1,0:T(8,128)(2,1)S(1)} %project.2), channel_id=1, source_target_pairs={{0,1},{1,0},{2,3},{3,2},{4,5},{5,4},{6,7},{7,6},{8,9},{9,8},{10,11... | collective-permute-start | bytes 3932168 | tf_op jit(solution)/shard_map/ppermute | solution.py:19
  351.9 8.5 %project.3 = bf16[512,1280]{1,0:T(8,128)(2,1)S(1)} custom-call(s32[4]{0:T(128)S(1)} %add_add_fusion.at_ref, bf16[512,640]{1,0:T(8,128)(2,1)S(1)} %copy-done, bf16[512,640]{1,0:T(8,128)(2,1)} %collective-permute-done.26.f1, bf16[512,640]{1,0:T(8,128)(2,1)S(1)} %copy-done.6, bf16[512,640]{1,0:T(8,128)(2,1)} %collective-permute-done.28.f3, ...), custom_call_target="tpu_custom_call" | custom-call | flops 3355443200 | bytes 10485760 | tf_op jit(solution)/shard_map/project/pallas_call | solution.py:378
  360.5 1.4 add_convert_fusion
  (110 shorter events, 18.1 us)
Async XLA Ops:
  0.8 4.5 %copy-start.10 = (bf16[512,1280]{1,0:T(8,128)(2,1)S(1)}, bf16[512,1280]{1,0:T(8,128)(2,1)}, u32[]{:S(2)}) copy-start(bf16[512,1280]{1,0:T(8,128)(2,1)} %refs_10_.1) | copy-start | bytes 3932164
  3.3 16.0 %collective-permute-start.1 = (bf16[512,640]{1,0:T(8,128)(2,1)S(1)}, bf16[512,640]{1,0:T(8,128)(2,1)S(1)}, u32[]{:S(2)}, u32[]{:S(2)}) collective-permute-start(bf16[512,640]{1,0:T(8,128)(2,1)S(1)} %get-tuple-element.38), channel_id=1, source_target_pairs={{0,64},{64,0},{1,65},{65,1},{2,66},{66,2},{3,67},{67,3},{4,68},{68... | collective-permute-start | bytes 1966088 | tf_op jit(solution)/shard_map/ppermute | solution.py:19
  5.4 28.0 %collective-permute-start = (bf16[512,640]{1,0:T(8,128)(2,1)S(1)}, bf16[512,640]{1,0:T(8,128)(2,1)S(1)}, u32[]{:S(2)}, u32[]{:S(2)}) collective-permute-start(bf16[512,640]{1,0:T(8,128)(2,1)S(1)} %constant_dynamic-slice_fusion.2), channel_id=1, source_target_pairs={{0,64},{64,0},{1,65},{65,1},{2,66},{66,2},{3,67},{67,3},{4,68},{68... | collective-permute-start | bytes 1966088 | tf_op jit(solution)/shard_map/ppermute | solution.py:19
  19.3 14.0 %copy-start.21 = (bf16[512,640]{1,0:T(8,128)(2,1)}, bf16[512,640]{1,0:T(8,128)(2,1)S(1)}, u32[]{:S(2)}) copy-start(bf16[512,640]{1,0:T(8,128)(2,1)S(1)} %collective-permute-done.1.tg_ref) | copy-start | bytes 1966084
  46.4 6.0 %copy-start.15 = (bf16[1280,160]{0,1:T(8,128)(2,1)S(1)}, bf16[1280,160]{0,1:T(8,128)(2,1)}, u32[]{:S(2)}) copy-start(bf16[1280,160]{0,1:T(8,128)(2,1)} %param.15) | copy-start | bytes 1228804
  48.0 23.9 %collective-permute-start.2 = (bf16[4,3,40,640]{3,2,1,0:T(8,128)(2,1)S(1)}, bf16[4,3,40,640]{3,2,1,0:T(8,128)(2,1)}, u32[]{:S(2)}, u32[]{:S(2)}) collective-permute-start(bf16[4,3,40,640]{3,2,1,0:T(8,128)(2,1)S(1)} %get-tuple-element.31), channel_id=1, source_target_pairs={{0,16},{16,32},{32,48},{48,0},{1,17},{17,33},{33,49},{49,1},{2,18}... | collective-permute-start | bytes 1843208 | tf_op jit(solution)/shard_map/ppermute | solution.py:19
  50.1 22.5 %collective-permute-start.3 = (bf16[4,3,40,640]{3,2,1,0:T(8,128)(2,1)S(1)}, bf16[4,3,40,640]{3,2,1,0:T(8,128)(2,1)}, u32[]{:S(2)}, u32[]{:S(2)}) collective-permute-start(bf16[4,3,40,640]{3,2,1,0:T(8,128)(2,1)S(1)} %get-tuple-element.33), channel_id=1, source_target_pairs={{0,48},{16,0},{32,16},{48,32},{1,49},{17,1},{33,17},{49,33},{2,50}... | collective-permute-start | bytes 1843208 | tf_op jit(solution)/shard_map/ppermute | solution.py:19
  52.3 15.8 %collective-permute-start.29 = (bf16[160,1280]{1,0:T(8,128)(2,1)S(1)}, bf16[160,1280]{1,0:T(8,128)(2,1)}, u32[]{:S(2)}, u32[]{:S(2)}) collective-permute-start(bf16[160,1280]{1,0:T(8,128)(2,1)S(1)} %bitcast.60), channel_id=1, source_target_pairs={{2,64},{66,2},{64,66},{3,65},{67,3},{65,67},{6,68},{70,6},{68,70},... | collective-permute-start | bytes 1228808 | tf_op jit(solution)/shard_map/ppermute | solution.py:24
  53.8 17.1 %collective-permute-start.30 = (bf16[160,1280]{1,0:T(8,128)(2,1)S(1)}, bf16[160,1280]{1,0:T(8,128)(2,1)}, u32[]{:S(2)}, u32[]{:S(2)}) collective-permute-start(bf16[160,1280]{1,0:T(8,128)(2,1)S(1)} %bitcast.61), channel_id=1, source_target_pairs={{2,0},{0,64},{64,2},{3,1},{1,65},{65,3},{6,4},{4,68},{68,6},{7,5},... | collective-permute-start | bytes 1228808 | tf_op jit(solution)/shard_map/ppermute | solution.py:24
  65.5 40.4 %collective-permute-start.15 = (bf16[3,3,512,128]{3,2,1,0:T(8,128)(2,1)}, bf16[3,3,512,128]{3,2,1,0:T(8,128)(2,1)S(1)}, u32[]{:S(2)}, u32[]{:S(2)}) collective-permute-start(bf16[3,3,512,128]{3,2,1,0:T(8,128)(2,1)} %get-tuple-element.21), channel_id=1, source_target_pairs={{0,4},{4,8},{8,12},{12,0},{1,5},{5,9},{9,13},{13,1},{2,6},{6,10},{... | collective-permute-start | bytes 3538952 | tf_op jit(solution)/shard_map/ppermute | solution.py:19
  66.9 4.0 %copy-start.20 = (bf16[3,3,512,128]{3,2,1,0:T(8,128)(2,1)S(1)}, bf16[3,3,512,128]{3,2,1,0:T(8,128)(2,1)}, u32[]{:S(2)}) copy-start(bf16[3,3,512,128]{3,2,1,0:T(8,128)(2,1)} %get-tuple-element.23) | copy-start | bytes 3538948
  68.2 50.5 %collective-permute-start.16 = (bf16[3,3,512,128]{3,2,1,0:T(8,128)(2,1)}, bf16[3,3,512,128]{3,2,1,0:T(8,128)(2,1)S(1)}, u32[]{:S(2)}, u32[]{:S(2)}) collective-permute-start(bf16[3,3,512,128]{3,2,1,0:T(8,128)(2,1)} %get-tuple-element.22), channel_id=1, source_target_pairs={{0,8},{4,12},{8,0},{12,4},{1,9},{5,13},{9,1},{13,5},{2,10},{6,14},... | collective-permute-start | bytes 3538952 | tf_op jit(solution)/shard_map/ppermute | solution.py:19
  70.9 50.3 %collective-permute-start.17 = (bf16[3,3,512,128]{3,2,1,0:T(8,128)(2,1)S(1)}, bf16[3,3,512,128]{3,2,1,0:T(8,128)(2,1)S(1)}, u32[]{:S(2)}, u32[]{:S(2)}) collective-permute-start(bf16[3,3,512,128]{3,2,1,0:T(8,128)(2,1)S(1)} %copy-done.20), channel_id=1, source_target_pairs={{0,12},{4,0},{8,4},{12,8},{1,13},{5,1},{9,5},{13,9},{2,14},{6,2},{... | collective-permute-start | bytes 3538952 | tf_op jit(solution)/shard_map/ppermute | solution.py:19
  71.9 33.9 %collective-permute-start.18 = (bf16[2,3,512,128]{3,2,1,0:T(8,128)(2,1)S(1)}, bf16[2,3,512,128]{3,2,1,0:T(8,128)(2,1)S(1)}, u32[]{:S(2)}, u32[]{:S(2)}) collective-permute-start(bf16[2,3,512,128]{3,2,1,0:T(8,128)(2,1)S(1)} %slice.74), channel_id=1, source_target_pairs={{8,24},{12,28},{24,40},{28,44},{40,56},{44,60},{56,72},{60,76},{72... | collective-permute-start | bytes 2359304 | tf_op jit(solution)/shard_map/ppermute | solution.py:30
  72.7 13.8 %collective-permute-start.4 = (bf16[4,3,40,640]{3,2,1,0:T(8,128)(2,1)S(1)}, bf16[4,3,40,640]{3,2,1,0:T(8,128)(2,1)S(1)}, u32[]{:S(2)}, u32[]{:S(2)}) collective-permute-start(bf16[4,3,40,640]{3,2,1,0:T(8,128)(2,1)S(1)} %get-tuple-element.32), channel_id=1, source_target_pairs={{0,32},{16,48},{32,0},{48,16},{1,33},{17,49},{33,1},{49,17},{2,34}... | collective-permute-start | bytes 1843208 | tf_op jit(solution)/shard_map/ppermute | solution.py:19
  86.4 43.5 %collective-permute-start.31 = (bf16[2,160,640]{2,1,0:T(8,128)(2,1)S(1)}, bf16[2,160,640]{2,1,0:T(8,128)(2,1)S(1)}, u32[]{:S(2)}, u32[]{:S(2)}) collective-permute-start(bf16[2,160,640]{2,1,0:T(8,128)(2,1)S(1)} %get-tuple-element.43), channel_id=1, source_target_pairs={{0,12},{4,0},{8,4},{12,8},{1,13},{5,1},{9,5},{13,9},{2,14},{6,2},{... | collective-permute-start | bytes 1228808 | tf_op jit(solution)/shard_map/ppermute | solution.py:19
  105.8 25.5 %collective-permute-start.5 = (bf16[3,40,640]{2,1,0:T(8,128)(2,1)S(1)}, bf16[3,40,640]{2,1,0:T(8,128)(2,1)S(1)}, u32[]{:S(2)}, u32[]{:S(2)}) collective-permute-start(bf16[3,40,640]{2,1,0:T(8,128)(2,1)S(1)} %get-tuple-element.44), channel_id=1, source_target_pairs={{0,4},{4,8},{8,12},{12,0},{1,5},{5,9},{9,13},{13,1},{2,6},{6,10},{... | collective-permute-start | bytes 460808 | tf_op jit(solution)/shard_map/ppermute | solution.py:19
  105.9 29.7 %collective-permute-start.6 = (bf16[3,40,640]{2,1,0:T(8,128)(2,1)S(1)}, bf16[3,40,640]{2,1,0:T(8,128)(2,1)S(1)}, u32[]{:S(2)}, u32[]{:S(2)}) collective-permute-start(bf16[3,40,640]{2,1,0:T(8,128)(2,1)S(1)} %get-tuple-element.46), channel_id=1, source_target_pairs={{0,12},{4,0},{8,4},{12,8},{1,13},{5,1},{9,5},{13,9},{2,14},{6,2},{... | collective-permute-start | bytes 460808 | tf_op jit(solution)/shard_map/ppermute | solution.py:19
  118.7 17.6 %collective-permute-start.7 = (bf16[3,40,640]{2,1,0:T(8,128)(2,1)S(1)}, bf16[3,40,640]{2,1,0:T(8,128)(2,1)S(1)}, u32[]{:S(2)}, u32[]{:S(2)}) collective-permute-start(bf16[3,40,640]{2,1,0:T(8,128)(2,1)S(1)} %get-tuple-element.45), channel_id=1, source_target_pairs={{0,8},{4,12},{8,0},{12,4},{1,9},{5,13},{9,1},{13,5},{2,10},{6,14},... | collective-permute-start | bytes 460808 | tf_op jit(solution)/shard_map/ppermute | solution.py:19
  121.2 16.1 %collective-permute-start.32 = (bf16[2,160,640]{2,1,0:T(8,128)(2,1)S(1)}, bf16[2,160,640]{2,1,0:T(8,128)(2,1)S(1)}, u32[]{:S(2)}, u32[]{:S(2)}) collective-permute-start(bf16[2,160,640]{2,1,0:T(8,128)(2,1)S(1)} %get-tuple-element.43), channel_id=1, source_target_pairs={{0,8},{4,12},{8,0},{12,4},{1,9},{5,13},{9,1},{13,5},{2,10},{6,14},... | collective-permute-start | bytes 1228808 | tf_op jit(solution)/shard_map/ppermute | solution.py:19
  122.2 23.6 %copy-start.9 = (bf16[512,1280]{1,0:T(8,128)(2,1)S(1)}, bf16[512,1280]{1,0:T(8,128)(2,1)}, u32[]{:S(2)}) copy-start(bf16[512,1280]{1,0:T(8,128)(2,1)} %q_ref.1) | copy-start | bytes 3932164
  130.0 26.5 %collective-permute-start.19 = (bf16[2,3,512,128]{3,2,1,0:T(8,128)(2,1)S(1)}, bf16[2,3,512,128]{3,2,1,0:T(8,128)(2,1)S(1)}, u32[]{:S(2)}, u32[]{:S(2)}) collective-permute-start(bf16[2,3,512,128]{3,2,1,0:T(8,128)(2,1)S(1)} %slice.96), channel_id=1, source_target_pairs={{0,16},{12,28},{16,32},{28,44},{32,48},{44,60},{48,64},{60,76},{64... | collective-permute-start | bytes 2359304 | tf_op jit(solution)/shard_map/ppermute | solution.py:30
  131.4 29.0 %collective-permute-start.20 = (bf16[2,3,512,128]{3,2,1,0:T(8,128)(2,1)S(1)}, bf16[2,3,512,128]{3,2,1,0:T(8,128)(2,1)S(1)}, u32[]{:S(2)}, u32[]{:S(2)}) collective-permute-start(bf16[2,3,512,128]{3,2,1,0:T(8,128)(2,1)S(1)} %slice.97), channel_id=1, source_target_pairs={{0,16},{4,20},{16,32},{20,36},{32,48},{36,52},{48,64},{52,68},{64,... | collective-permute-start | bytes 2359304 | tf_op jit(solution)/shard_map/ppermute | solution.py:30
  135.6 30.6 %collective-permute-start.21 = (bf16[2,3,512,128]{3,2,1,0:T(8,128)(2,1)S(1)}, bf16[2,3,512,128]{3,2,1,0:T(8,128)(2,1)S(1)}, u32[]{:S(2)}, u32[]{:S(2)}) collective-permute-start(bf16[2,3,512,128]{3,2,1,0:T(8,128)(2,1)S(1)} %slice.98), channel_id=1, source_target_pairs={{4,20},{8,24},{20,36},{24,40},{36,52},{40,56},{52,68},{56,72},{68,... | collective-permute-start | bytes 2359304 | tf_op jit(solution)/shard_map/ppermute | solution.py:30
  136.3 10.2 %collective-permute-start.33 = (bf16[2,160,640]{2,1,0:T(8,128)(2,1)S(1)}, bf16[2,160,640]{2,1,0:T(8,128)(2,1)S(1)}, u32[]{:S(2)}, u32[]{:S(2)}) collective-permute-start(bf16[2,160,640]{2,1,0:T(8,128)(2,1)S(1)} %get-tuple-element.43), channel_id=1, source_target_pairs={{0,4},{4,8},{8,12},{12,0},{1,5},{5,9},{9,13},{13,1},{2,6},{6,10},{... | collective-permute-start | bytes 1228808 | tf_op jit(solution)/shard_map/ppermute | solution.py:19
  137.2 11.3 %collective-permute-start.8 = (bf16[3,40,640]{2,1,0:T(8,128)(2,1)S(1)}, bf16[3,40,640]{2,1,0:T(8,128)(2,1)S(1)}, u32[]{:S(2)}, u32[]{:S(2)}) collective-permute-start(bf16[3,40,640]{2,1,0:T(8,128)(2,1)S(1)} %fusion.6), channel_id=1, source_target_pairs={{0,12},{4,0},{8,4},{12,8},{1,13},{5,1},{9,5},{13,9},{2,14},{6,2},{... | collective-permute-start | bytes 460808 | tf_op jit(solution)/shard_map/ppermute | solution.py:19
  146.6 6.4 %collective-permute-start.9 = (bf16[3,40,640]{2,1,0:T(8,128)(2,1)S(1)}, bf16[3,40,640]{2,1,0:T(8,128)(2,1)S(1)}, u32[]{:S(2)}, u32[]{:S(2)}) collective-permute-start(bf16[3,40,640]{2,1,0:T(8,128)(2,1)S(1)} %fusion.6), channel_id=1, source_target_pairs={{0,8},{4,12},{8,0},{12,4},{1,9},{5,13},{9,1},{13,5},{2,10},{6,14},... | collective-permute-start | bytes 460808 | tf_op jit(solution)/shard_map/ppermute | solution.py:19
  148.5 6.1 %collective-permute-start.10 = (bf16[3,40,640]{2,1,0:T(8,128)(2,1)S(1)}, bf16[3,40,640]{2,1,0:T(8,128)(2,1)S(1)}, u32[]{:S(2)}, u32[]{:S(2)}) collective-permute-start(bf16[3,40,640]{2,1,0:T(8,128)(2,1)S(1)} %fusion.6), channel_id=1, source_target_pairs={{0,4},{4,8},{8,12},{12,0},{1,5},{5,9},{9,13},{13,1},{2,6},{6,10},{... | collective-permute-start | bytes 460808 | tf_op jit(solution)/shard_map/ppermute | solution.py:19
  151.6 14.5 %copy-start.7 = (bf16[3,3,512,128]{3,2,1,0:T(8,128)(2,1)S(1)}, bf16[3,3,512,128]{3,2,1,0:T(8,128)(2,1)}, u32[]{:S(2)}) copy-start(bf16[3,3,512,128]{3,2,1,0:T(8,128)(2,1)} %get-tuple-element.20.g0) | copy-start | bytes 3538948
  151.6 14.5 %copy-start.8 = (s32[4]{0:T(128)S(1)}, s32[4]{0:T(128)}, u32[]{:S(2)}) copy-start(s32[4]{0:T(128)} %add_add_fusion.1.at_ref) | copy-start | bytes 52
  153.0 31.0 %collective-permute-start.38 = (bf16[2,160,640]{2,1,0:T(8,128)(2,1)S(1)}, bf16[2,160,640]{2,1,0:T(8,128)(2,1)S(1)}, u32[]{:S(2)}, u32[]{:S(2)}) collective-permute-start(bf16[2,160,640]{2,1,0:T(8,128)(2,1)S(1)} %get-tuple-element.42), channel_id=1, source_target_pairs={{0,48},{16,0},{32,16},{48,32},{1,49},{17,1},{33,17},{49,33},{2,50}... | collective-permute-start | bytes 1228808 | tf_op jit(solution)/shard_map/ppermute | solution.py:19
  154.6 29.4 %collective-permute-start.39 = (bf16[2,160,640]{2,1,0:T(8,128)(2,1)S(1)}, bf16[2,160,640]{2,1,0:T(8,128)(2,1)S(1)}, u32[]{:S(2)}, u32[]{:S(2)}) collective-permute-start(bf16[2,160,640]{2,1,0:T(8,128)(2,1)S(1)} %get-tuple-element.42), channel_id=1, source_target_pairs={{0,32},{16,48},{32,0},{48,16},{1,33},{17,49},{33,1},{49,17},{2,34}... | collective-permute-start | bytes 1228808 | tf_op jit(solution)/shard_map/ppermute | solution.py:19
  156.5 31.7 %collective-permute-start.40 = (bf16[2,160,640]{2,1,0:T(8,128)(2,1)S(1)}, bf16[2,160,640]{2,1,0:T(8,128)(2,1)S(1)}, u32[]{:S(2)}, u32[]{:S(2)}) collective-permute-start(bf16[2,160,640]{2,1,0:T(8,128)(2,1)S(1)} %get-tuple-element.42), channel_id=1, source_target_pairs={{0,16},{16,32},{32,48},{48,0},{1,17},{17,33},{33,49},{49,1},{2,18}... | collective-permute-start | bytes 1228808 | tf_op jit(solution)/shard_map/ppermute | solution.py:19
  160.3 27.8 %collective-permute-start.14 = (bf16[512,640]{1,0:T(8,128)(2,1)S(1)}, bf16[512,640]{1,0:T(8,128)(2,1)S(1)}, u32[]{:S(2)}, u32[]{:S(2)}) collective-permute-start(bf16[512,640]{1,0:T(8,128)(2,1)S(1)} %constant_dynamic-slice_fusion), channel_id=1, source_target_pairs={{0,64},{64,0},{1,65},{65,1},{2,66},{66,2},{3,67},{67,3},{4,68},{68... | collective-permute-start | bytes 1966088 | tf_op jit(solution)/shard_map/ppermute | solution.py:19
  166.2 22.0 %collective-permute-start.11 = (bf16[4,3,40,640]{3,2,1,0:T(8,128)(2,1)}, bf16[4,3,40,640]{3,2,1,0:T(8,128)(2,1)S(1)}, u32[]{:S(2)}, u32[]{:S(2)}) collective-permute-start(bf16[4,3,40,640]{3,2,1,0:T(8,128)(2,1)} %pad_maximum_fusion.2.g0), channel_id=1, source_target_pairs={{0,48},{16,0},{32,16},{48,32},{1,49},{17,1},{33,17},{49,33},{2,50}... | collective-permute-start | bytes 1843208 | tf_op jit(solution)/shard_map/ppermute | solution.py:19
  184.0 84.9 %collective-permute-start.34 = (bf16[4,2,160,640]{3,2,1,0:T(8,128)(2,1)S(1)}, bf16[4,2,160,640]{3,2,1,0:T(8,128)(2,1)}, u32[]{:S(2)}, u32[]{:S(2)}) collective-permute-start(bf16[4,2,160,640]{3,2,1,0:T(8,128)(2,1)S(1)} %pad_maximum_fusion.a0), channel_id=1, source_target_pairs={{0,48},{16,0},{32,16},{48,32},{1,49},{17,1},{33,17},{49,33},{2,50}... | collective-permute-start | bytes 4915208 | tf_op jit(solution)/shard_map/ppermute | solution.py:19
  184.1 11.1 %collective-permute-start.12 = (bf16[4,3,40,640]{3,2,1,0:T(8,128)(2,1)}, bf16[4,3,40,640]{3,2,1,0:T(8,128)(2,1)S(1)}, u32[]{:S(2)}, u32[]{:S(2)}) collective-permute-start(bf16[4,3,40,640]{3,2,1,0:T(8,128)(2,1)} %pad_maximum_fusion.2.g0), channel_id=1, source_target_pairs={{0,32},{16,48},{32,0},{48,16},{1,33},{17,49},{33,1},{49,17},{2,34}... | collective-permute-start | bytes 1843208 | tf_op jit(solution)/shard_map/ppermute | solution.py:19
  188.1 7.8 %collective-permute-start.22 = (bf16[3,512,128]{2,1,0:T(8,128)(2,1)S(1)}, bf16[3,512,128]{2,1,0:T(8,128)(2,1)S(1)}, u32[]{:S(2)}, u32[]{:S(2)}) collective-permute-start(bf16[3,512,128]{2,1,0:T(8,128)(2,1)S(1)} %get-tuple-element.36), channel_id=1, source_target_pairs={{0,12},{4,0},{8,4},{12,8},{1,13},{5,1},{9,5},{13,9},{2,14},{6,2},{... | collective-permute-start | bytes 1179656 | tf_op jit(solution)/shard_map/ppermute | solution.py:19
  188.1 2.5 copy-start.12
  188.1 105.7 %collective-permute-start.35 = (bf16[4,2,160,640]{3,2,1,0:T(8,128)(2,1)S(1)}, bf16[4,2,160,640]{3,2,1,0:T(8,128)(2,1)}, u32[]{:S(2)}, u32[]{:S(2)}) collective-permute-start(bf16[4,2,160,640]{3,2,1,0:T(8,128)(2,1)S(1)} %pad_maximum_fusion.a0), channel_id=1, source_target_pairs={{0,16},{16,32},{32,48},{48,0},{1,17},{17,33},{33,49},{49,1},{2,18}... | collective-permute-start | bytes 4915208 | tf_op jit(solution)/shard_map/ppermute | solution.py:19
  188.2 2.4 copy-start.13
  188.2 9.9 %collective-permute-start.23 = (bf16[3,512,128]{2,1,0:T(8,128)(2,1)S(1)}, bf16[3,512,128]{2,1,0:T(8,128)(2,1)S(1)}, u32[]{:S(2)}, u32[]{:S(2)}) collective-permute-start(bf16[3,512,128]{2,1,0:T(8,128)(2,1)S(1)} %get-tuple-element.35), channel_id=1, source_target_pairs={{0,8},{4,12},{8,0},{12,4},{1,9},{5,13},{9,1},{13,5},{2,10},{6,14},... | collective-permute-start | bytes 1179656 | tf_op jit(solution)/shard_map/ppermute | solution.py:19
  190.7 78.5 %copy-start.19 = (f32[1280]{0:T(1024)S(1)}, f32[1280]{0:T(1024)}, u32[]{:S(2)}) copy-start(f32[1280]{0:T(1024)} %param.14) | copy-start | bytes 15364
  195.1 107.8 %collective-permute-start.41 = (bf16[4,2,160,640]{3,2,1,0:T(8,128)(2,1)S(1)}, bf16[4,2,160,640]{3,2,1,0:T(8,128)(2,1)}, u32[]{:S(2)}, u32[]{:S(2)}) collective-permute-start(bf16[4,2,160,640]{3,2,1,0:T(8,128)(2,1)S(1)} %pad_maximum_fusion.1.b0), channel_id=1, source_target_pairs={{0,12},{4,0},{8,4},{12,8},{1,13},{5,1},{9,5},{13,9},{2,14},{6,2},{... | collective-permute-start | bytes 4915208 | tf_op jit(solution)/shard_map/ppermute | solution.py:19
  195.9 30.7 %copy-start.16 = (bf16[3,512,128]{2,1,0:T(8,128)(2,1)}, bf16[3,512,128]{2,1,0:T(8,128)(2,1)S(1)}, u32[]{:S(2)}) copy-start(bf16[3,512,128]{2,1,0:T(8,128)(2,1)S(1)} %collective-permute-done.22.r1) | copy-start | bytes 1179652
  195.9 109.2 %collective-permute-start.42 = (bf16[4,2,160,640]{3,2,1,0:T(8,128)(2,1)S(1)}, bf16[4,2,160,640]{3,2,1,0:T(8,128)(2,1)}, u32[]{:S(2)}, u32[]{:S(2)}) collective-permute-start(bf16[4,2,160,640]{3,2,1,0:T(8,128)(2,1)S(1)} %pad_maximum_fusion.1.b0), channel_id=1, source_target_pairs={{0,4},{4,8},{8,12},{12,0},{1,5},{5,9},{9,13},{13,1},{2,6},{6,10},{... | collective-permute-start | bytes 4915208 | tf_op jit(solution)/shard_map/ppermute | solution.py:19
  198.1 68.0 %copy-start.17 = (bf16[3,512,128]{2,1,0:T(8,128)(2,1)}, bf16[3,512,128]{2,1,0:T(8,128)(2,1)S(1)}, u32[]{:S(2)}) copy-start(bf16[3,512,128]{2,1,0:T(8,128)(2,1)S(1)} %collective-permute-done.23.r2) | copy-start | bytes 1179652
  198.1 28.5 %collective-permute-start.24 = (bf16[3,512,128]{2,1,0:T(8,128)(2,1)S(1)}, bf16[3,512,128]{2,1,0:T(8,128)(2,1)S(1)}, u32[]{:S(2)}, u32[]{:S(2)}) collective-permute-start(bf16[3,512,128]{2,1,0:T(8,128)(2,1)S(1)} %get-tuple-element.34), channel_id=1, source_target_pairs={{0,4},{4,8},{8,12},{12,0},{1,5},{5,9},{9,13},{13,1},{2,6},{6,10},{... | collective-permute-start | bytes 1179656 | tf_op jit(solution)/shard_map/ppermute | solution.py:19
  226.6 39.5 %copy-start.18 = (bf16[3,512,128]{2,1,0:T(8,128)(2,1)}, bf16[3,512,128]{2,1,0:T(8,128)(2,1)S(1)}, u32[]{:S(2)}) copy-start(bf16[3,512,128]{2,1,0:T(8,128)(2,1)S(1)} %collective-permute-done.24.r3) | copy-start | bytes 1179652
  226.6 51.2 %collective-permute-start.13 = (bf16[4,3,40,640]{3,2,1,0:T(8,128)(2,1)}, bf16[4,3,40,640]{3,2,1,0:T(8,128)(2,1)}, u32[]{:S(2)}, u32[]{:S(2)}) collective-permute-start(bf16[4,3,40,640]{3,2,1,0:T(8,128)(2,1)} %pad_maximum_fusion.2.g0), channel_id=1, source_target_pairs={{0,16},{16,32},{32,48},{48,0},{1,17},{17,33},{33,49},{49,1},{2,18}... | collective-permute-start | bytes 1843208 | tf_op jit(solution)/shard_map/ppermute | solution.py:19
  268.9 39.4 %collective-permute-start.25 = (bf16[512,640]{1,0:T(8,128)(2,1)}, bf16[512,640]{1,0:T(8,128)(2,1)S(1)}, u32[]{:S(2)}, u32[]{:S(2)}) collective-permute-start(bf16[512,640]{1,0:T(8,128)(2,1)} %get-tuple-element.26), channel_id=1, source_target_pairs={{0,64},{64,0},{1,65},{65,1},{2,66},{66,2},{3,67},{67,3},{4,68},{68... | collective-permute-start | bytes 1966088 | tf_op jit(solution)/shard_map/ppermute | solution.py:19
  277.8 36.0 %collective-permute-start.36 = (bf16[2,2,160,640]{3,2,1,0:T(8,128)(2,1)S(1)}, bf16[2,2,160,640]{3,2,1,0:T(8,128)(2,1)S(1)}, u32[]{:S(2)}, u32[]{:S(2)}) collective-permute-start(bf16[2,2,160,640]{3,2,1,0:T(8,128)(2,1)S(1)} %slice.105), channel_id=1, source_target_pairs={{0,48},{16,0},{32,16},{48,32},{1,49},{17,1},{33,17},{49,33},{2,50}... | collective-permute-start | bytes 2457608 | tf_op jit(solution)/shard_map/ppermute | solution.py:19
  293.9 15.9 %collective-permute-start.27 = (bf16[512,640]{1,0:T(8,128)(2,1)}, bf16[512,640]{1,0:T(8,128)(2,1)S(1)}, u32[]{:S(2)}, u32[]{:S(2)}) collective-permute-start(bf16[512,640]{1,0:T(8,128)(2,1)} %own.1.f0), channel_id=1, source_target_pairs={{0,2},{2,0},{1,3},{3,1},{4,6},{6,4},{5,7},{7,5},{8,10},{10,8},{9,1... | collective-permute-start | bytes 1966088 | tf_op jit(solution)/shard_map/ppermute | solution.py:19
  302.9 5.8 %copy-start.11 = (f32[512,640]{1,0:T(8,128)S(1)}, f32[512,640]{1,0:T(8,128)}, u32[]{:S(2)}) copy-start(f32[512,640]{1,0:T(8,128)} %get-tuple-element.25) | copy-start | bytes 3932164
  302.9 13.0 %collective-permute-start.37 = (bf16[2,2,160,640]{3,2,1,0:T(8,128)(2,1)}, bf16[2,2,160,640]{3,2,1,0:T(8,128)(2,1)}, u32[]{:S(2)}, u32[]{:S(2)}) collective-permute-start(bf16[2,2,160,640]{3,2,1,0:T(8,128)(2,1)} %slice.106), channel_id=1, source_target_pairs={{0,16},{16,32},{32,48},{48,0},{1,17},{17,33},{33,49},{49,1},{2,18}... | collective-permute-start | bytes 2457608 | tf_op jit(solution)/shard_map/ppermute | solution.py:19
  305.1 11.8 %collective-permute-start.43 = (bf16[2,2,160,640]{3,2,1,0:T(8,128)(2,1)}, bf16[2,2,160,640]{3,2,1,0:T(8,128)(2,1)}, u32[]{:S(2)}, u32[]{:S(2)}) collective-permute-start(bf16[2,2,160,640]{3,2,1,0:T(8,128)(2,1)} %slice.107), channel_id=1, source_target_pairs={{0,12},{4,0},{8,4},{12,8},{1,13},{5,1},{9,5},{13,9},{2,14},{6,2},{... | collective-permute-start | bytes 2457608 | tf_op jit(solution)/shard_map/ppermute | solution.py:19
  308.3 13.2 %collective-permute-start.44 = (bf16[2,2,160,640]{3,2,1,0:T(8,128)(2,1)}, bf16[2,2,160,640]{3,2,1,0:T(8,128)(2,1)}, u32[]{:S(2)}, u32[]{:S(2)}) collective-permute-start(bf16[2,2,160,640]{3,2,1,0:T(8,128)(2,1)} %slice.108), channel_id=1, source_target_pairs={{0,4},{4,8},{8,12},{12,0},{1,5},{5,9},{9,13},{13,1},{2,6},{6,10},{... | collective-permute-start | bytes 2457608 | tf_op jit(solution)/shard_map/ppermute | solution.py:19
  310.6 15.2 %collective-permute-start.26 = (bf16[512,640]{1,0:T(8,128)(2,1)}, bf16[512,640]{1,0:T(8,128)(2,1)}, u32[]{:S(2)}, u32[]{:S(2)}) collective-permute-start(bf16[512,640]{1,0:T(8,128)(2,1)} %add_convert_fusion.1), channel_id=1, source_target_pairs={{0,66},{64,0},{2,64},{66,2},{1,67},{65,1},{3,65},{67,3},{4,70},{68... | collective-permute-start | bytes 1966088 | tf_op jit(solution)/shard_map/ppermute | solution.py:24
  314.6 11.3 %collective-permute-start.28 = (bf16[512,640]{1,0:T(8,128)(2,1)}, bf16[512,640]{1,0:T(8,128)(2,1)}, u32[]{:S(2)}, u32[]{:S(2)}) collective-permute-start(bf16[512,640]{1,0:T(8,128)(2,1)} %add_convert_fusion.1), channel_id=1, source_target_pairs={{0,64},{64,2},{2,66},{66,0},{1,65},{65,3},{3,67},{67,1},{4,68},{68... | collective-permute-start | bytes 1966088 | tf_op jit(solution)/shard_map/ppermute | solution.py:24
  325.9 1.1 copy-start
  327.0 1.1 copy-start.2
  329.2 22.7 %copy-start.3 = (bf16[2,2,160,640]{3,2,1,0:T(8,128)(2,1)S(1)}, bf16[2,2,160,640]{3,2,1,0:T(8,128)(2,1)}, u32[]{:S(2)}) copy-start(bf16[2,2,160,640]{3,2,1,0:T(8,128)(2,1)} %copy-done.1) | copy-start | bytes 2457604
  329.2 22.7 %copy-start.6 = (bf16[512,640]{1,0:T(8,128)(2,1)S(1)}, bf16[512,640]{1,0:T(8,128)(2,1)}, u32[]{:S(2)}) copy-start(bf16[512,640]{1,0:T(8,128)(2,1)} %copy-done.4) | copy-start | bytes 1966084
  337.9 22.6 %collective-permute-start.45 = (bf16[512,1280]{1,0:T(8,128)(2,1)S(1)}, bf16[512,1280]{1,0:T(8,128)(2,1)S(1)}, u32[]{:S(2)}, u32[]{:S(2)}) collective-permute-start(bf16[512,1280]{1,0:T(8,128)(2,1)S(1)} %project.2), channel_id=1, source_target_pairs={{0,1},{1,0},{2,3},{3,2},{4,5},{5,4},{6,7},{7,6},{8,9},{9,8},{10,11... | collective-permute-start | bytes 3932168 | tf_op jit(solution)/shard_map/ppermute | solution.py:19
  (5 other events, 4.5 us)
where the time goes:
time: 363 us; the launch traced here: 362 us
  starting transfers between devices  146 us (40%)
  waiting for transfers between devices  115 us (32%)
  Pallas kernels  70.8 us (20%)
  local copies, waits for them, and re-layouts  20 us (6%)
  other arithmetic  10.1 us (3%)
    ppermute x38, starting transfers between devices, hop(): lax.ppermute(block, axis, [(i, (i + distance) % n) for i in range(n)])  129 us
    ppermute x38, waiting for transfers between devices, hop(): lax.ppermute(block, axis, [(i, (i + distance) % n) for i in range(n)])  108 us
    pallas_call x1, Pallas kernels, attend(): pl.pallas_call(functools.partial(attend_kernel, rows // 2), out_shape=jax...  17.7 us
    pallas_call x2, Pallas kernels, project(): pl.pallas_call(project_kernel, out_shape=jax.ShapeDtypeStruct((rows, 8 *...  17.2 us
    pallas_call x1, Pallas kernels, descent_of(): pl.pallas_call(descent_kernel, out_shape=out, grid_spec=pltpu.PrefetchSca...  12.2 us
    ppermute x4, starting transfers between devices, along_x(): lax.ppermute(block, ('xl', 'xh'), [(place[a], place[b]) for a, b in route])  10 us
    pallas_call x1, Pallas kernels, update_of(): pl.pallas_call(update_kernel, out_shape=shapes, grid_spec=pltpu.PrefetchS...  8.87 us
    slice x4, local copies, waits for them, and re-layouts, gather_ring(): return (block, up, down, hop(up[:2], axis, -1), hop(down[2:], axis, 1))  7.7 us
  transfers between devices with their start and end apart: 46, of which 19 were waited for; matrix products, arithmetic and copies ran while one was open for 5% of the time, Pallas kernels for 14%

commit v1 on v0

--- a/solution.py
+++ b/solution.py
@@ -1,4 +1,5 @@
 import functools
+import math
 
 import jax
 import jax.numpy as jnp
@@ -10,6 +11,7 @@
 
 AHD = 128
 EPS = 1e-06
+CUT = 6
 f32 = jnp.float32
 bf16 = jnp.bfloat16
 
@@ -144,7 +146,7 @@
     first = (xl == 0) & (z == 0)
     bias1 = jnp.where(first & (yb < 1), neg, f32(0))
     bias2 = jnp.where(first & (yb < 2), neg, f32(0))
-    scale = f32(1.0) / jnp.sqrt(f32(AHD))
+    scale = f32(math.log2(math.e) / math.sqrt(AHD))
     row = lax.broadcasted_iota(jnp.int32, (tile, tile), 0)
     col = lax.broadcasted_iota(jnp.int32, (tile, tile), 1)
     own = col <= row
@@ -156,7 +158,7 @@
         q = q_ref[yb, slot, here, :]
 
         def score(d, cols):
-            return dot(q, kv_ref[yb + 2 - d, 0, slot, cols, :], 1, 1) * scale
+            return dot(q, kv_ref[yb + 2 - d, 0, slot, cols, :], 1, 1)
 
         def weigh(p, d, cols):
             return dot(p.astype(bf16), kv_ref[yb + 2 - d, 1, slot, cols, :], 1, 0)
@@ -167,7 +169,7 @@
         s2 = score(edge, other) + jnp.where(t == 0, bias2, f32(0))
         top = jnp.maximum(jnp.max(s0, axis=1, keepdims=True), jnp.max(s1, axis=1, keepdims=True))
         top = jnp.maximum(top, jnp.max(s2, axis=1, keepdims=True))
-        p0, p1, p2 = jnp.exp(s0 - top), jnp.exp(s1 - top), jnp.exp(s2 - top)
+        p0, p1, p2 = (jnp.exp2((s - top) * scale) for s in (s0, s1, s2))
         total = sum(jnp.sum(p, axis=1, keepdims=True) for p in (p0, p1, p2))
         out = weigh(jnp.where(own, p0, 0.0), 0, here) + weigh(jnp.where(own, 0.0, p0), 2, here)
         out += weigh(p1, 1, slice(None)) + weigh(p2, edge, other)
@@ -320,7 +322,10 @@
     )(at, u, queries, gain, attn)
 
 
-def project_kernel(at_ref, f0, f1, f2, f3, a0, a1, a3, a2a, a2b, b0, b1, b3, b2a, b2b, out_ref, w_ref, f_ref, sem):
+def project_kernel(at_ref, f0, f1, f2, f3, *refs):
+    lefts, rights = refs[:8], refs[8:16]
+    a0, b0 = lefts[0], rights[0]
+    out_ref, w_ref, f_ref, sem = refs[16:]
     z, y, core, x = at_ref[0], at_ref[1], at_ref[2], at_ref[3]
     width, cut = a0.shape[2], a0.shape[3]
     full = cut + b0.shape[3]
@@ -334,15 +339,14 @@
     for i in range(4):
         for j in range(4):
             for half, (big, small) in enumerate(((z, y), (y, z))):
-                far = (a2a, b2a) if j < 2 else (a2b, b2b)
-                srcs = ((a0, a1, far[0], a3), (b0, b1, far[1], b3))[half]
+                src = (lefts, rights)[half][2 * i + j // 2]
                 p, q = lax.rem(big + i, 4), lax.rem(small + j, 4)
                 zb, yb = (p, q) if half == 0 else (q, p)
 
                 @pl.when(zb // 2 == core)
                 def _():
                     for g in range(2):
-                        copy(srcs[i].at[j - 2 if i == 2 and j >= 2 else j, g], half, g, zb, yb).start()
+                        copy(src.at[j % 2, g], half, g, zb, yb).start()
 
     for r, f in enumerate((f0, f1, f2, f3)):
         cols = pl.multiple_of(lax.rem(x + r, 4) * f.shape[1], AHD)
@@ -378,7 +382,7 @@
     return pl.pallas_call(
         project_kernel,
         out_shape=jax.ShapeDtypeStruct((rows, 8 * width), bf16),
-        in_specs=[pl.BlockSpec(memory_space=pltpu.SMEM), *[vmem] * 4, *[hbm] * 10],
+        in_specs=[pl.BlockSpec(memory_space=pltpu.SMEM), *[vmem] * 4, *[hbm] * 16],
         out_specs=vmem,
         scratch_shapes=[
             pltpu.VMEM((8 * width, full), bf16),
@@ -406,9 +410,12 @@
     return [block, got[1], got[2], got[3]]
 
 
-def gather_ring(block, axis):
-    up, down = hop(block, axis, -1), hop(block, axis, 1)
-    return (block, up, down, hop(up[:2], axis, -1), hop(down[2:], axis, 1))
+def gather_ring(parts, axis):
+    low, high = jnp.stack(parts[:2]), jnp.stack(parts[2:])
+    up_low, down_high = hop(low, axis, -1), hop(high, axis, 1)
+    up_high, down_low = hop(high, axis, -1), hop(low, axis, 1)
+    far_low, far_high = hop(up_low, axis, -1), hop(down_high, axis, 1)
+    return (low, high, up_low, up_high, far_low, far_high, down_low, down_high)
 
 
 def body(queries, keys, values, token_rate, head_rate, fast_weights, ttt_gain, out_weight):
@@ -439,8 +446,9 @@
     low = jnp.where(x == 0, turned, jnp.where(x == 3, two, one))
     high = jnp.where(x == 3, turned, jnp.where(x == 0, one, two))
     pair = jnp.stack([low, high])
-    block_a = jnp.stack(gather(pair[:, :, :width], "y"))
-    block_b = jnp.stack(gather(pair[:, :, width:], "z"))
+    cut = CUT * AHD
+    block_a = gather(pair[:, :, :cut], "y")
+    block_b = gather(pair[:, :, cut:], "z")
     queries_far = lax.optimization_barrier((queries, t_got))[0]
     q_got = hop(cols_of(queries_far, 1 - xl), "xl", 1)
 

time: 363 us -> 310 us (0.85)
  starting transfers between devices: 146 us -> 115 us
  waiting for transfers between devices: 115 us -> 97.9 us
  local copies, waits for them, and re-layouts: 20 us -> 12 us
    ppermute x38 -> x42, starting transfers between devices: 129 us -> 91.4 us  [hop(): lax.ppermute(block, axis, [(i, (i + distance) % n) for i in range(n)])]
    ppermute x38 -> x42, waiting for transfers between devices: 108 us -> 70.7 us  [hop(): lax.ppermute(block, axis, [(i, (i + distance) % n) for i in range(n)])]
    ppermute x4, waiting for transfers between devices: 4.48 us -> 18.4 us  [along_x(): lax.ppermute(block, ('xl', 'xh'), [(place[a], place[b]) for a, b in route])]
    slice x4 -> x0, local copies, waits for them, and re-layouts: 7.7 us -> none  [gather_ring(): return (block, up, down, hop(up[:2], axis, -1), hop(down[2:], axis, 1))]
    ppermute x4, waiting for transfers between devices: 2.67 us -> 8.82 us  [next_ring(): return lax.ppermute(block, axes, route)]
    ppermute x4, starting transfers between devices: 10 us -> 15 us  [along_x(): lax.ppermute(block, ('xl', 'xh'), [(place[a], place[b]) for a, b in route])]
    unnamed x46 -> x62, local copies, waits for them, and re-layouts: 6.79 us -> 8.62 us
  transfers between devices with their start and end apart: 46 -> 50, of which waited for: 19 -> 14; matrix products, arithmetic and copies ran while one was open for 5% -> 4% of each run, Pallas kernels for 14% -> 21%
where the time goes in v1:
time: 310 us; the launch traced here: 309 us
  starting transfers between devices  115 us (37%)
  waiting for transfers between devices  97.9 us (32%)
  Pallas kernels  72.6 us (23%)
  local copies, waits for them, and re-layouts  12 us (4%)
  other arithmetic  10.6 us (3%)
    ppermute x42, starting transfers between devices, hop(): lax.ppermute(block, axis, [(i, (i + distance) % n) for i in range(n)])  91.4 us
    ppermute x42, waiting for transfers between devices, hop(): lax.ppermute(block, axis, [(i, (i + distance) % n) for i in range(n)])  70.7 us
    pallas_call x2, Pallas kernels, project(): pl.pallas_call(project_kernel, out_shape=jax.ShapeDtypeStruct((rows, 8 *...  18.8 us
    ppermute x4, waiting for transfers between devices, along_x(): lax.ppermute(block, ('xl', 'xh'), [(place[a], place[b]) for a, b in route])  18.4 us
    pallas_call x1, Pallas kernels, attend(): pl.pallas_call(functools.partial(attend_kernel, rows // 2), out_shape=jax...  17.6 us
    ppermute x4, starting transfers between devices, along_x(): lax.ppermute(block, ('xl', 'xh'), [(place[a], place[b]) for a, b in route])  15 us
    pallas_call x1, Pallas kernels, descent_of(): pl.pallas_call(descent_kernel, out_shape=out, grid_spec=pltpu.PrefetchSca...  12.2 us
    pallas_call x1, Pallas kernels, update_of(): pl.pallas_call(update_kernel, out_shape=shapes, grid_spec=pltpu.PrefetchS...  8.87 us
  transfers between devices with their start and end apart: 50, of which 14 were waited for; matrix products, arithmetic and copies ran while one was open for 4% of the time, Pallas kernels for 21%

profile of v1, /device:TPU:1, one launch (start us, length us, event | category | flops | bytes accessed | tf_op | source)
XLA Modules:
  0.0 308.7 jit_solution(15639897005158134830)
XLA Ops:
  0.0 1.4 collective-permute-start.29
  1.4 6.3 %collective-permute-start.30 = (bf16[160,1280]{1,0:T(8,128)(2,1)}, bf16[160,1280]{1,0:T(8,128)(2,1)}, u32[]{:S(2)}, u32[]{:S(2)}) collective-permute-start(bf16[160,1280]{1,0:T(8,128)(2,1)} %bitcast.64), channel_id=1, source_target_pairs={{2,0},{0,64},{64,2},{3,1},{1,65},{65,3},{6,4},{4,68},{68,6},{7,5},... | collective-permute-start | bytes 1228808 | tf_op jit(solution)/shard_map/ppermute | solution.py:26
  8.3 6.4 %pack.1 = (bf16[3,3,512,128]{3,2,1,0:T(8,128)(2,1)}, bf16[3,3,512,128]{3,2,1,0:T(8,128)(2,1)}, bf16[3,3,512,128]{3,2,1,0:T(8,128)(2,1)}, bf16[3,3,512,128]{3,2,1,0:T(8,128)(2,1)}) custom-call(s32[4]{0:T(128)} %add_add_fusion.1.at_ref, bf16[512,1280]{1,0:T(8,128)(2,1)} %q_ref.1, bf16[512,1280]{1,0:T(8,128)(2,1)} %refs_10_.1, bf16[512,1280]{1,0:T(8,128)(2,1)} %refs_11_.1, ...), custom_call_target="tpu_custom_call" | custom-call | bytes 10485760 | tf_op jit(solution)/shard_map/pack/pallas_call | solution.py:111
  14.7 1.4 collective-permute-start.15
  16.1 1.2 multiply_convert_fusion
  17.7 1.2 collective-permute-start
  18.9 1.3 select_bitcast_fusion
  20.9 3.6 %collective-permute-start.41 = (bf16[2,160,512]{2,1,0:T(8,128)(2,1)}, bf16[2,160,512]{2,1,0:T(8,128)(2,1)S(1)}, u32[]{:S(2)}, u32[]{:S(2)}) collective-permute-start(bf16[2,160,512]{2,1,0:T(8,128)(2,1)} %pad_maximum_fusion.5), channel_id=1, source_target_pairs={{0,32},{16,48},{32,0},{48,16},{1,33},{17,49},{33,1},{49,17},{2,34}... | collective-permute-start | bytes 983048 | tf_op jit(solution)/shard_map/ppermute | solution.py:21
  25.3 6.9 %collective-permute-done.1.tg_ref = bf16[512,640]{1,0:T(8,128)(2,1)} collective-permute-done((bf16[512,640]{1,0:T(8,128)(2,1)S(1)}, bf16[512,640]{1,0:T(8,128)(2,1)}, u32[]{:S(2)}, u32[]{:S(2)}) %collective-permute-start.1) | collective-permute-done | bytes 655392 | tf_op jit(solution)/shard_map/ppermute | solution.py:21
  32.1 2.6 collective-permute-start.16
  34.8 11.4 %collective-permute-done.kg_ref = bf16[512,640]{1,0:T(8,128)(2,1)} collective-permute-done((bf16[512,640]{1,0:T(8,128)(2,1)S(1)}, bf16[512,640]{1,0:T(8,128)(2,1)}, u32[]{:S(2)}, u32[]{:S(2)}) %collective-permute-start) | collective-permute-done | bytes 655392 | tf_op jit(solution)/shard_map/ppermute | solution.py:21
  46.2 1.6 collective-permute-start.17
  48.5 3.8 %collective-permute-start.40 = (bf16[2,160,512]{2,1,0:T(8,128)(2,1)}, bf16[2,160,512]{2,1,0:T(8,128)(2,1)S(1)}, u32[]{:S(2)}, u32[]{:S(2)}) collective-permute-start(bf16[2,160,512]{2,1,0:T(8,128)(2,1)} %pad_maximum_fusion.5), channel_id=1, source_target_pairs={{0,48},{16,0},{32,16},{48,32},{1,49},{17,1},{33,17},{49,33},{2,50}... | collective-permute-start | bytes 983048 | tf_op jit(solution)/shard_map/ppermute | solution.py:21
  52.4 12.2 %descent.1 = bf16[4,4,3,40,640]{4,3,2,1,0:T(8,128)(2,1)} custom-call(s32[4]{0:T(128)} %add_add_fusion.1.at_ref, bf16[512,1280]{1,0:T(8,128)(2,1)} %refs_10_.1, bf16[512,640]{1,0:T(8,128)(2,1)} %get-tuple-element.39.t_ref, bf16[512,640]{1,0:T(8,128)(2,1)} %collective-permute-done.kg_ref, bf16[512,640]{1,0:T(8,128)(2,1)} %collective-permute-done.1.tg_ref, ...), custom_call_target="tpu_custom_call" | custom-call | flops 5033164800 | bytes 8388608 | tf_op jit(solution)/shard_map/descent/pallas_call | solution.py:71
  64.6 1.6 slice_bitcast_fusion.2
  66.3 2.7 collective-permute-start.3
  69.0 2.9 collective-permute-start.32
  72.0 17.3 %collective-permute-done.17.g3 = bf16[3,3,512,128]{3,2,1,0:T(8,128)(2,1)S(1)} collective-permute-done((bf16[3,3,512,128]{3,2,1,0:T(8,128)(2,1)}, bf16[3,3,512,128]{3,2,1,0:T(8,128)(2,1)S(1)}, u32[]{:S(2)}, u32[]{:S(2)}) %collective-permute-start.17) | collective-permute-done | bytes 1179680 | tf_op jit(solution)/shard_map/ppermute | solution.py:21
  89.3 3.7 %collective-permute-start.33 = (bf16[2,160,768]{2,1,0:T(8,128)(2,1)S(1)}, bf16[2,160,768]{2,1,0:T(8,128)(2,1)S(1)}, u32[]{:S(2)}, u32[]{:S(2)}) collective-permute-start(bf16[2,160,768]{2,1,0:T(8,128)(2,1)S(1)} %fusion.3), channel_id=1, source_target_pairs={{0,4},{4,8},{8,12},{12,0},{1,5},{5,9},{9,13},{13,1},{2,6},{6,10},{... | collective-permute-start | bytes 1474568 | tf_op jit(solution)/shard_map/ppermute | solution.py:21
  93.3 1.3 collective-permute-start.31
  94.6 3.5 %collective-permute-start.14 = (bf16[512,640]{1,0:T(8,128)(2,1)S(1)}, bf16[512,640]{1,0:T(8,128)(2,1)S(1)}, u32[]{:S(2)}, u32[]{:S(2)}) collective-permute-start(bf16[512,640]{1,0:T(8,128)(2,1)S(1)} %constant_dynamic-slice_fusion), channel_id=1, source_target_pairs={{0,64},{64,0},{1,65},{65,1},{2,66},{66,2},{3,67},{67,3},{4,68},{68... | collective-permute-start | bytes 1966088 | tf_op jit(solution)/shard_map/ppermute | solution.py:21
  98.1 3.6 %collective-permute-start.19 = (bf16[2,3,512,128]{3,2,1,0:T(8,128)(2,1)S(1)}, bf16[2,3,512,128]{3,2,1,0:T(8,128)(2,1)S(1)}, u32[]{:S(2)}, u32[]{:S(2)}) collective-permute-start(bf16[2,3,512,128]{3,2,1,0:T(8,128)(2,1)S(1)} %slice.80), channel_id=1, source_target_pairs={{0,16},{12,28},{16,32},{28,44},{32,48},{44,60},{48,64},{60,76},{64... | collective-permute-start | bytes 2359304 | tf_op jit(solution)/shard_map/ppermute | solution.py:32
  101.7 3.5 %collective-permute-start.20 = (bf16[2,3,512,128]{3,2,1,0:T(8,128)(2,1)S(1)}, bf16[2,3,512,128]{3,2,1,0:T(8,128)(2,1)S(1)}, u32[]{:S(2)}, u32[]{:S(2)}) collective-permute-start(bf16[2,3,512,128]{3,2,1,0:T(8,128)(2,1)S(1)} %slice.81), channel_id=1, source_target_pairs={{0,16},{4,20},{16,32},{20,36},{32,48},{36,52},{48,64},{52,68},{64,... | collective-permute-start | bytes 2359304 | tf_op jit(solution)/shard_map/ppermute | solution.py:32
  105.3 1.4 fusion.2
  107.4 1.6 collective-permute-start.5
  109.1 1.0 pad_maximum_fusion.3.refs_9_
  110.2 1.4 collective-permute-start.6
  111.5 1.4 collective-permute-done.5
  113.0 0.8 collective-permute-start.7
  114.3 4.2 %collective-permute-done.7 = bf16[3,40,640]{2,1,0:T(8,128)(2,1)S(1)} collective-permute-done((bf16[3,40,640]{2,1,0:T(8,128)(2,1)S(1)}, bf16[3,40,640]{2,1,0:T(8,128)(2,1)S(1)}, u32[]{:S(2)}, u32[]{:S(2)}) %collective-permute-start.7) | collective-permute-done | bytes 153632 | tf_op jit(solution)/shard_map/ppermute | solution.py:21
  118.6 2.1 collective-permute-start.43
  120.7 8.8 %collective-permute-done.20.h2 = bf16[2,3,512,128]{3,2,1,0:T(8,128)(2,1)S(1)} collective-permute-done((bf16[2,3,512,128]{3,2,1,0:T(8,128)(2,1)S(1)}, bf16[2,3,512,128]{3,2,1,0:T(8,128)(2,1)S(1)}, u32[]{:S(2)}, u32[]{:S(2)}) %collective-permute-start.20) | collective-permute-done | bytes 786464 | tf_op jit(solution)/shard_map/ppermute | solution.py:32
  129.6 2.4 collective-permute-start.37
  132.1 17.6 %attend.1 = bf16[4,3,512,128]{3,2,1,0:T(8,128)(2,1)S(1)} custom-call(s32[4]{0:T(128)S(1)} %copy-done.17, bf16[3,3,512,128]{3,2,1,0:T(8,128)(2,1)S(1)} %copy-done.14, bf16[3,3,512,128]{3,2,1,0:T(8,128)(2,1)S(1)} %copy-done.16, bf16[3,3,512,128]{3,2,1,0:T(8,128)(2,1)S(1)} %collective-permute-done.16.g2, ...), custom_call_target="tpu_custom_call" | custom-call | flops 4026531840 | bytes 12582912 | tf_op jit(solution)/shard_map/attend/pallas_call | solution.py:185
  149.7 13.3 %collective-permute-start.34 = (bf16[2,2,160,768]{3,2,1,0:T(8,128)(2,1)S(1)}, bf16[2,2,160,768]{3,2,1,0:T(8,128)(2,1)}, u32[]{:S(2)}, u32[]{:S(2)}) collective-permute-start(bf16[2,2,160,768]{3,2,1,0:T(8,128)(2,1)S(1)} %pad_maximum_fusion.refs_0_), channel_id=1, source_target_pairs={{0,48},{16,0},{32,16},{48,32},{1,49},{17,1},{33,17},{49,33},{2,50}... | collective-permute-start | bytes 2949128 | tf_op jit(solution)/shard_map/ppermute | solution.py:21
  163.0 2.7 collective-permute-start.8
  166.4 0.8 slice_bitcast_fusion.4
  167.2 2.3 collective-permute-done.8
  169.5 3.1 %collective-permute-start.22 = (bf16[3,512,128]{2,1,0:T(8,128)(2,1)S(1)}, bf16[3,512,128]{2,1,0:T(8,128)(2,1)S(1)}, u32[]{:S(2)}, u32[]{:S(2)}) collective-permute-start(bf16[3,512,128]{2,1,0:T(8,128)(2,1)S(1)} %get-tuple-element.36), channel_id=1, source_target_pairs={{0,12},{4,0},{8,4},{12,8},{1,13},{5,1},{9,5},{13,9},{2,14},{6,2},{... | collective-permute-start | bytes 1179656 | tf_op jit(solution)/shard_map/ppermute | solution.py:21
  173.9 11.4 %collective-permute-done.22.r1 = bf16[3,512,128]{2,1,0:T(8,128)(2,1)S(1)} collective-permute-done((bf16[3,512,128]{2,1,0:T(8,128)(2,1)S(1)}, bf16[3,512,128]{2,1,0:T(8,128)(2,1)S(1)}, u32[]{:S(2)}, u32[]{:S(2)}) %collective-permute-start.22) | collective-permute-done | bytes 393248 | tf_op jit(solution)/shard_map/ppermute | solution.py:21
  185.7 3.6 %collective-permute-done.24.r3 = bf16[3,512,128]{2,1,0:T(8,128)(2,1)S(1)} collective-permute-done((bf16[3,512,128]{2,1,0:T(8,128)(2,1)S(1)}, bf16[3,512,128]{2,1,0:T(8,128)(2,1)S(1)}, u32[]{:S(2)}, u32[]{:S(2)}) %collective-permute-start.24) | collective-permute-done | bytes 393248 | tf_op jit(solution)/shard_map/ppermute | solution.py:21
  190.0 2.8 columns.1
  192.8 2.6 collective-permute-start.25
  196.2 2.2 collective-permute-start.47
  198.3 9.8 %collective-permute-done.13.g3 = bf16[4,3,40,640]{3,2,1,0:T(8,128)(2,1)} collective-permute-done((bf16[4,3,40,640]{3,2,1,0:T(8,128)(2,1)S(1)}, bf16[4,3,40,640]{3,2,1,0:T(8,128)(2,1)}, u32[]{:S(2)}, u32[]{:S(2)}) %collective-permute-start.13) | collective-permute-done | bytes 614432 | tf_op jit(solution)/shard_map/ppermute | solution.py:21
  208.1 5.6 %collective-permute-start.45 = (bf16[2,2,160,512]{3,2,1,0:T(8,128)(2,1)}, bf16[2,2,160,512]{3,2,1,0:T(8,128)(2,1)S(1)}, u32[]{:S(2)}, u32[]{:S(2)}) collective-permute-start(bf16[2,2,160,512]{3,2,1,0:T(8,128)(2,1)} %collective-permute-done.43.refs_10_), channel_id=1, source_target_pairs={{0,12},{4,0},{8,4},{12,8},{1,13},{5,1},{9,5},{13,9},{2,14},{6,2},{... | collective-permute-start | bytes 1966088 | tf_op jit(solution)/shard_map/ppermute | solution.py:21
  214.3 8.9 %update.1 = (bf16[3,640,640]{2,1,0:T(8,128)(2,1)}, f32[512,640]{1,0:T(8,128)}) custom-call(s32[4]{0:T(128)} %add_add_fusion.1.at_ref, f32[2]{0:T(128)} %rate_ref.1, bf16[4,3,40,640]{3,2,1,0:T(8,128)(2,1)} %copy-done.22, bf16[4,3,40,640]{3,2,1,0:T(8,128)(2,1)} %collective-permute-done.11.g1, bf16[4,3,40,640]{3,2,1,0:T(8,128)(2,1)} %collective-permute-done.12.g2, ...), custom_call_target="tpu_custom_call" | custom-call | flops 1258291200 | bytes 8388608 | tf_op jit(solution)/shard_map/update/pallas_call | solution.py:274
  223.2 15.3 %collective-permute-start.38 = (bf16[2,2,160,768]{3,2,1,0:T(8,128)(2,1)}, bf16[2,2,160,768]{3,2,1,0:T(8,128)(2,1)}, u32[]{:S(2)}, u32[]{:S(2)}) collective-permute-start(bf16[2,2,160,768]{3,2,1,0:T(8,128)(2,1)} %collective-permute-done.37.refs_7_), channel_id=1, source_target_pairs={{0,16},{16,32},{32,48},{48,0},{1,17},{17,33},{33,49},{49,1},{2,18}... | collective-permute-start | bytes 2949128 | tf_op jit(solution)/shard_map/ppermute | solution.py:21
  238.5 5.9 %own.1.f0 = bf16[512,640]{1,0:T(8,128)(2,1)} custom-call(s32[4]{0:T(128)} %add_add_fusion.1.at_ref, bf16[3,640,640]{2,1,0:T(8,128)(2,1)} %get-tuple-element.19.u_ref, bf16[512,1280]{1,0:T(8,128)(2,1)} %q_ref.1, f32[1,1280]{1,0:T(1,128)} %broadcast_in_dim.3.gain_ref, bf16[512,640]{1,0:T(8,128)(2,1)} %get-tuple-element.24.attn_ref), custom_call_target="tpu_custom_call" | custom-call | flops 1258291200 | bytes 6291456 | tf_op jit(solution)/shard_map/own/pallas_call | solution.py:303
  244.4 1.0 add_convert_fusion.1
  245.7 0.9 copy-done.9
  246.6 7.4 %collective-permute-start.26 = (bf16[512,640]{1,0:T(8,128)(2,1)}, bf16[512,640]{1,0:T(8,128)(2,1)}, u32[]{:S(2)}, u32[]{:S(2)}) collective-permute-start(bf16[512,640]{1,0:T(8,128)(2,1)} %add_convert_fusion.1), channel_id=1, source_target_pairs={{0,66},{64,0},{2,64},{66,2},{1,67},{65,1},{3,65},{67,3},{4,70},{68... | collective-permute-start | bytes 1966088 | tf_op jit(solution)/shard_map/ppermute | solution.py:26
  253.9 0.9 copy-done.11
  254.9 1.8 collective-permute-done.27.f2
  256.7 18.4 %collective-permute-done.26.f1 = bf16[512,640]{1,0:T(8,128)(2,1)} collective-permute-done((bf16[512,640]{1,0:T(8,128)(2,1)}, bf16[512,640]{1,0:T(8,128)(2,1)}, u32[]{:S(2)}, u32[]{:S(2)}) %collective-permute-start.26) | collective-permute-done | bytes 655392 | tf_op jit(solution)/shard_map/ppermute | solution.py:26
  275.1 1.1 copy-done.2
  276.2 1.1 copy-done.4
  277.3 1.1 copy-done.7
  278.4 1.1 copy-done.10
  279.5 1.1 copy-done.12
  280.6 9.0 %project.2 = bf16[512,1280]{1,0:T(8,128)(2,1)} custom-call(s32[4]{0:T(128)S(1)} %add_add_fusion.2.at_ref, bf16[512,640]{1,0:T(8,128)(2,1)S(1)} %copy-done, bf16[512,640]{1,0:T(8,128)(2,1)} %collective-permute-done.26.f1, bf16[512,640]{1,0:T(8,128)(2,1)} %collective-permute-done.27.f2, bf16[512,640]{1,0:T(8,128)(2,1)} %collective-permute-done.28.f3, ...), custom_call_target="tpu_custom_call" | custom-call | flops 3355443200 | bytes 10485760 | tf_op jit(solution)/shard_map/project/pallas_call | solution.py:382
  289.6 6.4 %collective-permute-start.49 = (bf16[512,1280]{1,0:T(8,128)(2,1)}, bf16[512,1280]{1,0:T(8,128)(2,1)S(1)}, u32[]{:S(2)}, u32[]{:S(2)}) collective-permute-start(bf16[512,1280]{1,0:T(8,128)(2,1)} %project.2), channel_id=1, source_target_pairs={{0,1},{1,0},{2,3},{3,2},{4,5},{5,4},{6,7},{7,6},{8,9},{9,8},{10,11... | collective-permute-start | bytes 3932168 | tf_op jit(solution)/shard_map/ppermute | solution.py:21
  296.1 9.8 %project.3 = bf16[512,1280]{1,0:T(8,128)(2,1)} custom-call(s32[4]{0:T(128)S(1)} %add_add_fusion.at_ref, bf16[512,640]{1,0:T(8,128)(2,1)S(1)} %copy-done, bf16[512,640]{1,0:T(8,128)(2,1)} %collective-permute-done.26.f1, bf16[512,640]{1,0:T(8,128)(2,1)} %collective-permute-done.27.f2, bf16[512,640]{1,0:T(8,128)(2,1)} %collective-permute-done.28.f3, ...), custom_call_target="tpu_custom_call" | custom-call | flops 3355443200 | bytes 10485760 | tf_op jit(solution)/shard_map/project/pallas_call | solution.py:382
  306.0 2.7 add_convert_fusion
  (135 shorter events, 10.1 us)
Async XLA Ops:
  0.0 18.9 %collective-permute-start.29 = (bf16[160,1280]{1,0:T(8,128)(2,1)}, bf16[160,1280]{1,0:T(8,128)(2,1)}, u32[]{:S(2)}, u32[]{:S(2)}) collective-permute-start(bf16[160,1280]{1,0:T(8,128)(2,1)} %bitcast.63), channel_id=1, source_target_pairs={{2,64},{66,2},{64,66},{3,65},{67,3},{65,67},{6,68},{70,6},{68,70},... | collective-permute-start | bytes 1228808 | tf_op jit(solution)/shard_map/ppermute | solution.py:26
  1.4 17.5 %collective-permute-start.30 = (bf16[160,1280]{1,0:T(8,128)(2,1)}, bf16[160,1280]{1,0:T(8,128)(2,1)}, u32[]{:S(2)}, u32[]{:S(2)}) collective-permute-start(bf16[160,1280]{1,0:T(8,128)(2,1)} %bitcast.64), channel_id=1, source_target_pairs={{2,0},{0,64},{64,2},{3,1},{1,65},{65,3},{6,4},{4,68},{68,6},{7,5},... | collective-permute-start | bytes 1228808 | tf_op jit(solution)/shard_map/ppermute | solution.py:26
  8.3 7.7 %copy-start.30 = (f32[512,2]{0,1:T(2,128)S(1)}, f32[512,2]{0,1:T(2,128)}, u32[]{:S(2)}) copy-start(f32[512,2]{0,1:T(2,128)} %param.11) | copy-start | bytes 12292
  8.3 7.8 %copy-start.19 = (bf16[512,1280]{1,0:T(8,128)(2,1)S(1)}, bf16[512,1280]{1,0:T(8,128)(2,1)}, u32[]{:S(2)}) copy-start(bf16[512,1280]{1,0:T(8,128)(2,1)} %refs_11_.1) | copy-start | bytes 3932164
  14.7 54.3 %collective-permute-start.15 = (bf16[3,3,512,128]{3,2,1,0:T(8,128)(2,1)}, bf16[3,3,512,128]{3,2,1,0:T(8,128)(2,1)S(1)}, u32[]{:S(2)}, u32[]{:S(2)}) collective-permute-start(bf16[3,3,512,128]{3,2,1,0:T(8,128)(2,1)} %get-tuple-element.21), channel_id=1, source_target_pairs={{0,4},{4,8},{8,12},{12,0},{1,5},{5,9},{9,13},{13,1},{2,6},{6,10},{... | collective-permute-start | bytes 3538952 | tf_op jit(solution)/shard_map/ppermute | solution.py:21
  17.3 14.9 %collective-permute-start.1 = (bf16[512,640]{1,0:T(8,128)(2,1)S(1)}, bf16[512,640]{1,0:T(8,128)(2,1)}, u32[]{:S(2)}, u32[]{:S(2)}) collective-permute-start(bf16[512,640]{1,0:T(8,128)(2,1)S(1)} %get-tuple-element.38), channel_id=1, source_target_pairs={{0,64},{64,0},{1,65},{65,1},{2,66},{66,2},{3,67},{67,3},{4,68},{68... | collective-permute-start | bytes 1966088 | tf_op jit(solution)/shard_map/ppermute | solution.py:21
  17.7 28.5 %collective-permute-start = (bf16[512,640]{1,0:T(8,128)(2,1)S(1)}, bf16[512,640]{1,0:T(8,128)(2,1)}, u32[]{:S(2)}, u32[]{:S(2)}) collective-permute-start(bf16[512,640]{1,0:T(8,128)(2,1)S(1)} %constant_dynamic-slice_fusion.2), channel_id=1, source_target_pairs={{0,64},{64,0},{1,65},{65,1},{2,66},{66,2},{3,67},{67,3},{4,68},{68... | collective-permute-start | bytes 1966088 | tf_op jit(solution)/shard_map/ppermute | solution.py:21
  18.9 28.9 %copy-start.14 = (bf16[3,3,512,128]{3,2,1,0:T(8,128)(2,1)S(1)}, bf16[3,3,512,128]{3,2,1,0:T(8,128)(2,1)}, u32[]{:S(2)}) copy-start(bf16[3,3,512,128]{3,2,1,0:T(8,128)(2,1)} %get-tuple-element.20.g0) | copy-start | bytes 3538948
  20.9 26.9 %collective-permute-start.41 = (bf16[2,160,512]{2,1,0:T(8,128)(2,1)}, bf16[2,160,512]{2,1,0:T(8,128)(2,1)S(1)}, u32[]{:S(2)}, u32[]{:S(2)}) collective-permute-start(bf16[2,160,512]{2,1,0:T(8,128)(2,1)} %pad_maximum_fusion.5), channel_id=1, source_target_pairs={{0,32},{16,48},{32,0},{48,16},{1,33},{17,49},{33,1},{49,17},{2,34}... | collective-permute-start | bytes 983048 | tf_op jit(solution)/shard_map/ppermute | solution.py:21
  24.5 24.0 %collective-permute-start.42 = (bf16[2,160,512]{2,1,0:T(8,128)(2,1)}, bf16[2,160,512]{2,1,0:T(8,128)(2,1)}, u32[]{:S(2)}, u32[]{:S(2)}) collective-permute-start(bf16[2,160,512]{2,1,0:T(8,128)(2,1)} %pad_maximum_fusion.5), channel_id=1, source_target_pairs={{0,16},{16,32},{32,48},{48,0},{1,17},{17,33},{33,49},{49,1},{2,18}... | collective-permute-start | bytes 983048 | tf_op jit(solution)/shard_map/ppermute | solution.py:21
  32.1 36.9 %collective-permute-start.16 = (bf16[3,3,512,128]{3,2,1,0:T(8,128)(2,1)}, bf16[3,3,512,128]{3,2,1,0:T(8,128)(2,1)S(1)}, u32[]{:S(2)}, u32[]{:S(2)}) collective-permute-start(bf16[3,3,512,128]{3,2,1,0:T(8,128)(2,1)} %get-tuple-element.22), channel_id=1, source_target_pairs={{0,8},{4,12},{8,0},{12,4},{1,9},{5,13},{9,1},{13,5},{2,10},{6,14},... | collective-permute-start | bytes 3538952 | tf_op jit(solution)/shard_map/ppermute | solution.py:21
  46.2 43.1 %collective-permute-start.17 = (bf16[3,3,512,128]{3,2,1,0:T(8,128)(2,1)}, bf16[3,3,512,128]{3,2,1,0:T(8,128)(2,1)S(1)}, u32[]{:S(2)}, u32[]{:S(2)}) collective-permute-start(bf16[3,3,512,128]{3,2,1,0:T(8,128)(2,1)} %get-tuple-element.23), channel_id=1, source_target_pairs={{0,12},{4,0},{8,4},{12,8},{1,13},{5,1},{9,5},{13,9},{2,14},{6,2},{... | collective-permute-start | bytes 3538952 | tf_op jit(solution)/shard_map/ppermute | solution.py:21
  47.8 18.5 %collective-permute-start.18 = (bf16[2,3,512,128]{3,2,1,0:T(8,128)(2,1)S(1)}, bf16[2,3,512,128]{3,2,1,0:T(8,128)(2,1)S(1)}, u32[]{:S(2)}, u32[]{:S(2)}) collective-permute-start(bf16[2,3,512,128]{3,2,1,0:T(8,128)(2,1)S(1)} %slice.62), channel_id=1, source_target_pairs={{8,24},{12,28},{24,40},{28,44},{40,56},{44,60},{56,72},{60,76},{72... | collective-permute-start | bytes 2359304 | tf_op jit(solution)/shard_map/ppermute | solution.py:32
  48.5 17.7 %collective-permute-start.40 = (bf16[2,160,512]{2,1,0:T(8,128)(2,1)}, bf16[2,160,512]{2,1,0:T(8,128)(2,1)S(1)}, u32[]{:S(2)}, u32[]{:S(2)}) collective-permute-start(bf16[2,160,512]{2,1,0:T(8,128)(2,1)} %pad_maximum_fusion.5), channel_id=1, source_target_pairs={{0,48},{16,0},{32,16},{48,32},{1,49},{17,1},{33,17},{49,33},{2,50}... | collective-permute-start | bytes 983048 | tf_op jit(solution)/shard_map/ppermute | solution.py:21
  66.2 28.4 %collective-permute-start.2 = (bf16[4,3,40,640]{3,2,1,0:T(8,128)(2,1)S(1)}, bf16[4,3,40,640]{3,2,1,0:T(8,128)(2,1)S(1)}, u32[]{:S(2)}, u32[]{:S(2)}) collective-permute-start(bf16[4,3,40,640]{3,2,1,0:T(8,128)(2,1)S(1)} %get-tuple-element.31), channel_id=1, source_target_pairs={{0,16},{16,32},{32,48},{48,0},{1,17},{17,33},{33,49},{49,1},{2,18}... | collective-permute-start | bytes 1843208 | tf_op jit(solution)/shard_map/ppermute | solution.py:21
  66.3 31.8 %collective-permute-start.3 = (bf16[4,3,40,640]{3,2,1,0:T(8,128)(2,1)S(1)}, bf16[4,3,40,640]{3,2,1,0:T(8,128)(2,1)S(1)}, u32[]{:S(2)}, u32[]{:S(2)}) collective-permute-start(bf16[4,3,40,640]{3,2,1,0:T(8,128)(2,1)S(1)} %get-tuple-element.33), channel_id=1, source_target_pairs={{0,48},{16,0},{32,16},{48,32},{1,49},{17,1},{33,17},{49,33},{2,50}... | collective-permute-start | bytes 1843208 | tf_op jit(solution)/shard_map/ppermute | solution.py:21
  69.0 24.2 %copy-start.15 = (bf16[3,3,512,128]{3,2,1,0:T(8,128)(2,1)}, bf16[3,3,512,128]{3,2,1,0:T(8,128)(2,1)S(1)}, u32[]{:S(2)}) copy-start(bf16[3,3,512,128]{3,2,1,0:T(8,128)(2,1)S(1)} %collective-permute-done.15.g1) | copy-start | bytes 3538948
  69.0 24.1 %copy-start.18 = (bf16[512,1280]{1,0:T(8,128)(2,1)S(1)}, bf16[512,1280]{1,0:T(8,128)(2,1)}, u32[]{:S(2)}) copy-start(bf16[512,1280]{1,0:T(8,128)(2,1)} %q_ref.1) | copy-start | bytes 3932164
  69.0 32.7 %collective-permute-start.4 = (bf16[4,3,40,640]{3,2,1,0:T(8,128)(2,1)S(1)}, bf16[4,3,40,640]{3,2,1,0:T(8,128)(2,1)S(1)}, u32[]{:S(2)}, u32[]{:S(2)}) collective-permute-start(bf16[4,3,40,640]{3,2,1,0:T(8,128)(2,1)S(1)} %get-tuple-element.32), channel_id=1, source_target_pairs={{0,32},{16,48},{32,0},{48,16},{1,33},{17,49},{33,1},{49,17},{2,34}... | collective-permute-start | bytes 1843208 | tf_op jit(solution)/shard_map/ppermute | solution.py:21
  69.0 24.3 %collective-permute-start.32 = (bf16[2,160,768]{2,1,0:T(8,128)(2,1)S(1)}, bf16[2,160,768]{2,1,0:T(8,128)(2,1)S(1)}, u32[]{:S(2)}, u32[]{:S(2)}) collective-permute-start(bf16[2,160,768]{2,1,0:T(8,128)(2,1)S(1)} %fusion.3), channel_id=1, source_target_pairs={{0,8},{4,12},{8,0},{12,4},{1,9},{5,13},{9,1},{13,5},{2,10},{6,14},... | collective-permute-start | bytes 1474568 | tf_op jit(solution)/shard_map/ppermute | solution.py:21
  89.3 17.4 %collective-permute-start.33 = (bf16[2,160,768]{2,1,0:T(8,128)(2,1)S(1)}, bf16[2,160,768]{2,1,0:T(8,128)(2,1)S(1)}, u32[]{:S(2)}, u32[]{:S(2)}) collective-permute-start(bf16[2,160,768]{2,1,0:T(8,128)(2,1)S(1)} %fusion.3), channel_id=1, source_target_pairs={{0,4},{4,8},{8,12},{12,0},{1,5},{5,9},{9,13},{13,1},{2,6},{6,10},{... | collective-permute-start | bytes 1474568 | tf_op jit(solution)/shard_map/ppermute | solution.py:21
  93.3 14.1 %collective-permute-start.31 = (bf16[2,160,768]{2,1,0:T(8,128)(2,1)S(1)}, bf16[2,160,768]{2,1,0:T(8,128)(2,1)S(1)}, u32[]{:S(2)}, u32[]{:S(2)}) collective-permute-start(bf16[2,160,768]{2,1,0:T(8,128)(2,1)S(1)} %fusion.3), channel_id=1, source_target_pairs={{0,12},{4,0},{8,4},{12,8},{1,13},{5,1},{9,5},{13,9},{2,14},{6,2},{... | collective-permute-start | bytes 1474568 | tf_op jit(solution)/shard_map/ppermute | solution.py:21
  94.6 15.5 %collective-permute-start.14 = (bf16[512,640]{1,0:T(8,128)(2,1)S(1)}, bf16[512,640]{1,0:T(8,128)(2,1)S(1)}, u32[]{:S(2)}, u32[]{:S(2)}) collective-permute-start(bf16[512,640]{1,0:T(8,128)(2,1)S(1)} %constant_dynamic-slice_fusion), channel_id=1, source_target_pairs={{0,64},{64,0},{1,65},{65,1},{2,66},{66,2},{3,67},{67,3},{4,68},{68... | collective-permute-start | bytes 1966088 | tf_op jit(solution)/shard_map/ppermute | solution.py:21
  98.1 20.4 %collective-permute-start.19 = (bf16[2,3,512,128]{3,2,1,0:T(8,128)(2,1)S(1)}, bf16[2,3,512,128]{3,2,1,0:T(8,128)(2,1)S(1)}, u32[]{:S(2)}, u32[]{:S(2)}) collective-permute-start(bf16[2,3,512,128]{3,2,1,0:T(8,128)(2,1)S(1)} %slice.80), channel_id=1, source_target_pairs={{0,16},{12,28},{16,32},{28,44},{32,48},{44,60},{48,64},{60,76},{64... | collective-permute-start | bytes 2359304 | tf_op jit(solution)/shard_map/ppermute | solution.py:32
  101.7 27.8 %collective-permute-start.20 = (bf16[2,3,512,128]{3,2,1,0:T(8,128)(2,1)S(1)}, bf16[2,3,512,128]{3,2,1,0:T(8,128)(2,1)S(1)}, u32[]{:S(2)}, u32[]{:S(2)}) collective-permute-start(bf16[2,3,512,128]{3,2,1,0:T(8,128)(2,1)S(1)} %slice.81), channel_id=1, source_target_pairs={{0,16},{4,20},{16,32},{20,36},{32,48},{36,52},{48,64},{52,68},{64,... | collective-permute-start | bytes 2359304 | tf_op jit(solution)/shard_map/ppermute | solution.py:32
  106.7 22.9 %collective-permute-start.21 = (bf16[2,3,512,128]{3,2,1,0:T(8,128)(2,1)S(1)}, bf16[2,3,512,128]{3,2,1,0:T(8,128)(2,1)S(1)}, u32[]{:S(2)}, u32[]{:S(2)}) collective-permute-start(bf16[2,3,512,128]{3,2,1,0:T(8,128)(2,1)S(1)} %slice.82), channel_id=1, source_target_pairs={{4,20},{8,24},{20,36},{24,40},{36,52},{40,56},{52,68},{56,72},{68,... | collective-permute-start | bytes 2359304 | tf_op jit(solution)/shard_map/ppermute | solution.py:32
  107.4 5.5 %collective-permute-start.5 = (bf16[3,40,640]{2,1,0:T(8,128)(2,1)S(1)}, bf16[3,40,640]{2,1,0:T(8,128)(2,1)S(1)}, u32[]{:S(2)}, u32[]{:S(2)}) collective-permute-start(bf16[3,40,640]{2,1,0:T(8,128)(2,1)S(1)} %get-tuple-element.42), channel_id=1, source_target_pairs={{0,4},{4,8},{8,12},{12,0},{1,5},{5,9},{9,13},{13,1},{2,6},{6,10},{... | collective-permute-start | bytes 460808 | tf_op jit(solution)/shard_map/ppermute | solution.py:21
  110.2 4.1 %collective-permute-start.6 = (bf16[3,40,640]{2,1,0:T(8,128)(2,1)S(1)}, bf16[3,40,640]{2,1,0:T(8,128)(2,1)S(1)}, u32[]{:S(2)}, u32[]{:S(2)}) collective-permute-start(bf16[3,40,640]{2,1,0:T(8,128)(2,1)S(1)} %get-tuple-element.44), channel_id=1, source_target_pairs={{0,12},{4,0},{8,4},{12,8},{1,13},{5,1},{9,5},{13,9},{2,14},{6,2},{... | collective-permute-start | bytes 460808 | tf_op jit(solution)/shard_map/ppermute | solution.py:21
  113.0 5.6 %collective-permute-start.7 = (bf16[3,40,640]{2,1,0:T(8,128)(2,1)S(1)}, bf16[3,40,640]{2,1,0:T(8,128)(2,1)S(1)}, u32[]{:S(2)}, u32[]{:S(2)}) collective-permute-start(bf16[3,40,640]{2,1,0:T(8,128)(2,1)S(1)} %get-tuple-element.43), channel_id=1, source_target_pairs={{0,8},{4,12},{8,0},{12,4},{1,9},{5,13},{9,1},{13,5},{2,10},{6,14},... | collective-permute-start | bytes 460808 | tf_op jit(solution)/shard_map/ppermute | solution.py:21
  113.8 15.8 %copy-start.1 = (bf16[2,2,160,512]{3,2,1,0:T(8,128)(2,1)}, bf16[2,2,160,512]{3,2,1,0:T(8,128)(2,1)S(1)}, u32[]{:S(2)}) copy-start(bf16[2,2,160,512]{3,2,1,0:T(8,128)(2,1)S(1)} %pad_maximum_fusion.2.refs_8_) | copy-start | bytes 1966084
  114.3 35.4 %collective-permute-start.46 = (bf16[2,2,160,512]{3,2,1,0:T(8,128)(2,1)S(1)}, bf16[2,2,160,512]{3,2,1,0:T(8,128)(2,1)}, u32[]{:S(2)}, u32[]{:S(2)}) collective-permute-start(bf16[2,2,160,512]{3,2,1,0:T(8,128)(2,1)S(1)} %pad_maximum_fusion.3.refs_9_), channel_id=1, source_target_pairs={{0,4},{4,8},{8,12},{12,0},{1,5},{5,9},{9,13},{13,1},{2,6},{6,10},{... | collective-permute-start | bytes 1966088 | tf_op jit(solution)/shard_map/ppermute | solution.py:21
  118.6 47.2 %collective-permute-start.44 = (bf16[2,2,160,512]{3,2,1,0:T(8,128)(2,1)S(1)}, bf16[2,2,160,512]{3,2,1,0:T(8,128)(2,1)S(1)}, u32[]{:S(2)}, u32[]{:S(2)}) collective-permute-start(bf16[2,2,160,512]{3,2,1,0:T(8,128)(2,1)S(1)} %pad_maximum_fusion.3.refs_9_), channel_id=1, source_target_pairs={{0,12},{4,0},{8,4},{12,8},{1,13},{5,1},{9,5},{13,9},{2,14},{6,2},{... | collective-permute-start | bytes 1966088 | tf_op jit(solution)/shard_map/ppermute | solution.py:21
  118.6 44.5 %collective-permute-start.43 = (bf16[2,2,160,512]{3,2,1,0:T(8,128)(2,1)S(1)}, bf16[2,2,160,512]{3,2,1,0:T(8,128)(2,1)}, u32[]{:S(2)}, u32[]{:S(2)}) collective-permute-start(bf16[2,2,160,512]{3,2,1,0:T(8,128)(2,1)S(1)} %pad_maximum_fusion.2.refs_8_), channel_id=1, source_target_pairs={{0,12},{4,0},{8,4},{12,8},{1,13},{5,1},{9,5},{13,9},{2,14},{6,2},{... | collective-permute-start | bytes 1966088 | tf_op jit(solution)/shard_map/ppermute | solution.py:21
  129.5 36.2 %collective-permute-start.48 = (bf16[2,2,160,512]{3,2,1,0:T(8,128)(2,1)S(1)}, bf16[2,2,160,512]{3,2,1,0:T(8,128)(2,1)S(1)}, u32[]{:S(2)}, u32[]{:S(2)}) collective-permute-start(bf16[2,2,160,512]{3,2,1,0:T(8,128)(2,1)S(1)} %pad_maximum_fusion.2.refs_8_), channel_id=1, source_target_pairs={{0,4},{4,8},{8,12},{12,0},{1,5},{5,9},{9,13},{13,1},{2,6},{6,10},{... | collective-permute-start | bytes 1966088 | tf_op jit(solution)/shard_map/ppermute | solution.py:21
  129.6 43.7 %collective-permute-start.37 = (bf16[2,2,160,768]{3,2,1,0:T(8,128)(2,1)S(1)}, bf16[2,2,160,768]{3,2,1,0:T(8,128)(2,1)}, u32[]{:S(2)}, u32[]{:S(2)}) collective-permute-start(bf16[2,2,160,768]{3,2,1,0:T(8,128)(2,1)S(1)} %pad_maximum_fusion.1.refs_1_), channel_id=1, source_target_pairs={{0,16},{16,32},{32,48},{48,0},{1,17},{17,33},{33,49},{49,1},{2,18}... | collective-permute-start | bytes 2949128 | tf_op jit(solution)/shard_map/ppermute | solution.py:21
  149.7 43.1 %collective-permute-start.34 = (bf16[2,2,160,768]{3,2,1,0:T(8,128)(2,1)S(1)}, bf16[2,2,160,768]{3,2,1,0:T(8,128)(2,1)}, u32[]{:S(2)}, u32[]{:S(2)}) collective-permute-start(bf16[2,2,160,768]{3,2,1,0:T(8,128)(2,1)S(1)} %pad_maximum_fusion.refs_0_), channel_id=1, source_target_pairs={{0,48},{16,0},{32,16},{48,32},{1,49},{17,1},{33,17},{49,33},{2,50}... | collective-permute-start | bytes 2949128 | tf_op jit(solution)/shard_map/ppermute | solution.py:21
  163.0 6.5 %collective-permute-start.8 = (bf16[3,40,640]{2,1,0:T(8,128)(2,1)S(1)}, bf16[3,40,640]{2,1,0:T(8,128)(2,1)S(1)}, u32[]{:S(2)}, u32[]{:S(2)}) collective-permute-start(bf16[3,40,640]{2,1,0:T(8,128)(2,1)S(1)} %fusion.6), channel_id=1, source_target_pairs={{0,12},{4,0},{8,4},{12,8},{1,13},{5,1},{9,5},{13,9},{2,14},{6,2},{... | collective-permute-start | bytes 460808 | tf_op jit(solution)/shard_map/ppermute | solution.py:21
  165.7 6.9 %collective-permute-start.9 = (bf16[3,40,640]{2,1,0:T(8,128)(2,1)S(1)}, bf16[3,40,640]{2,1,0:T(8,128)(2,1)S(1)}, u32[]{:S(2)}, u32[]{:S(2)}) collective-permute-start(bf16[3,40,640]{2,1,0:T(8,128)(2,1)S(1)} %fusion.6), channel_id=1, source_target_pairs={{0,8},{4,12},{8,0},{12,4},{1,9},{5,13},{9,1},{13,5},{2,10},{6,14},... | collective-permute-start | bytes 460808 | tf_op jit(solution)/shard_map/ppermute | solution.py:21
  165.7 7.0 %collective-permute-start.10 = (bf16[3,40,640]{2,1,0:T(8,128)(2,1)S(1)}, bf16[3,40,640]{2,1,0:T(8,128)(2,1)S(1)}, u32[]{:S(2)}, u32[]{:S(2)}) collective-permute-start(bf16[3,40,640]{2,1,0:T(8,128)(2,1)S(1)} %fusion.6), channel_id=1, source_target_pairs={{0,4},{4,8},{8,12},{12,0},{1,5},{5,9},{9,13},{13,1},{2,6},{6,10},{... | collective-permute-start | bytes 460808 | tf_op jit(solution)/shard_map/ppermute | solution.py:21
  169.5 15.8 %collective-permute-start.22 = (bf16[3,512,128]{2,1,0:T(8,128)(2,1)S(1)}, bf16[3,512,128]{2,1,0:T(8,128)(2,1)S(1)}, u32[]{:S(2)}, u32[]{:S(2)}) collective-permute-start(bf16[3,512,128]{2,1,0:T(8,128)(2,1)S(1)} %get-tuple-element.36), channel_id=1, source_target_pairs={{0,12},{4,0},{8,4},{12,8},{1,13},{5,1},{9,5},{13,9},{2,14},{6,2},{... | collective-permute-start | bytes 1179656 | tf_op jit(solution)/shard_map/ppermute | solution.py:21
  172.6 12.7 %collective-permute-start.23 = (bf16[3,512,128]{2,1,0:T(8,128)(2,1)S(1)}, bf16[3,512,128]{2,1,0:T(8,128)(2,1)S(1)}, u32[]{:S(2)}, u32[]{:S(2)}) collective-permute-start(bf16[3,512,128]{2,1,0:T(8,128)(2,1)S(1)} %get-tuple-element.35), channel_id=1, source_target_pairs={{0,8},{4,12},{8,0},{12,4},{1,9},{5,13},{9,1},{13,5},{2,10},{6,14},... | collective-permute-start | bytes 1179656 | tf_op jit(solution)/shard_map/ppermute | solution.py:21
  172.7 16.5 %collective-permute-start.24 = (bf16[3,512,128]{2,1,0:T(8,128)(2,1)S(1)}, bf16[3,512,128]{2,1,0:T(8,128)(2,1)S(1)}, u32[]{:S(2)}, u32[]{:S(2)}) collective-permute-start(bf16[3,512,128]{2,1,0:T(8,128)(2,1)S(1)} %get-tuple-element.34), channel_id=1, source_target_pairs={{0,4},{4,8},{8,12},{12,0},{1,5},{5,9},{9,13},{13,1},{2,6},{6,10},{... | collective-permute-start | bytes 1179656 | tf_op jit(solution)/shard_map/ppermute | solution.py:21
  173.2 40.5 %copy-start.29 = (f32[1280]{0:T(1024)S(1)}, f32[1280]{0:T(1024)}, u32[]{:S(2)}) copy-start(f32[1280]{0:T(1024)} %param.14) | copy-start | bytes 15364
  173.3 41.0 %copy-start.22 = (bf16[4,3,40,640]{3,2,1,0:T(8,128)(2,1)}, bf16[4,3,40,640]{3,2,1,0:T(8,128)(2,1)S(1)}, u32[]{:S(2)}) copy-start(bf16[4,3,40,640]{3,2,1,0:T(8,128)(2,1)S(1)} %pad_maximum_fusion.4.g0) | copy-start | bytes 1843204
  173.3 22.1 %collective-permute-start.11 = (bf16[4,3,40,640]{3,2,1,0:T(8,128)(2,1)S(1)}, bf16[4,3,40,640]{3,2,1,0:T(8,128)(2,1)}, u32[]{:S(2)}, u32[]{:S(2)}) collective-permute-start(bf16[4,3,40,640]{3,2,1,0:T(8,128)(2,1)S(1)} %pad_maximum_fusion.4.g0), channel_id=1, source_target_pairs={{0,48},{16,0},{32,16},{48,32},{1,49},{17,1},{33,17},{49,33},{2,50}... | collective-permute-start | bytes 1843208 | tf_op jit(solution)/shard_map/ppermute | solution.py:21
  185.3 37.9 %collective-permute-start.35 = (bf16[2,2,160,768]{3,2,1,0:T(8,128)(2,1)S(1)}, bf16[2,2,160,768]{3,2,1,0:T(8,128)(2,1)}, u32[]{:S(2)}, u32[]{:S(2)}) collective-permute-start(bf16[2,2,160,768]{3,2,1,0:T(8,128)(2,1)S(1)} %pad_maximum_fusion.1.refs_1_), channel_id=1, source_target_pairs={{0,48},{16,0},{32,16},{48,32},{1,49},{17,1},{33,17},{49,33},{2,50}... | collective-permute-start | bytes 2949128 | tf_op jit(solution)/shard_map/ppermute | solution.py:21
  185.3 4.0 %copy-start.27 = (bf16[3,512,128]{2,1,0:T(8,128)(2,1)}, bf16[3,512,128]{2,1,0:T(8,128)(2,1)S(1)}, u32[]{:S(2)}) copy-start(bf16[3,512,128]{2,1,0:T(8,128)(2,1)S(1)} %collective-permute-done.23.r2) | copy-start | bytes 1179652
  185.3 10.8 %collective-permute-start.12 = (bf16[4,3,40,640]{3,2,1,0:T(8,128)(2,1)S(1)}, bf16[4,3,40,640]{3,2,1,0:T(8,128)(2,1)}, u32[]{:S(2)}, u32[]{:S(2)}) collective-permute-start(bf16[4,3,40,640]{3,2,1,0:T(8,128)(2,1)S(1)} %pad_maximum_fusion.4.g0), channel_id=1, source_target_pairs={{0,32},{16,48},{32,0},{48,16},{1,33},{17,49},{33,1},{49,17},{2,34}... | collective-permute-start | bytes 1843208 | tf_op jit(solution)/shard_map/ppermute | solution.py:21
  189.3 18.8 %collective-permute-start.13 = (bf16[4,3,40,640]{3,2,1,0:T(8,128)(2,1)S(1)}, bf16[4,3,40,640]{3,2,1,0:T(8,128)(2,1)}, u32[]{:S(2)}, u32[]{:S(2)}) collective-permute-start(bf16[4,3,40,640]{3,2,1,0:T(8,128)(2,1)S(1)} %pad_maximum_fusion.4.g0), channel_id=1, source_target_pairs={{0,16},{16,32},{32,48},{48,0},{1,17},{17,33},{33,49},{49,1},{2,18}... | collective-permute-start | bytes 1843208 | tf_op jit(solution)/shard_map/ppermute | solution.py:21
  192.8 45.7 %collective-permute-start.25 = (bf16[512,640]{1,0:T(8,128)(2,1)}, bf16[512,640]{1,0:T(8,128)(2,1)S(1)}, u32[]{:S(2)}, u32[]{:S(2)}) collective-permute-start(bf16[512,640]{1,0:T(8,128)(2,1)} %get-tuple-element.26), channel_id=1, source_target_pairs={{0,64},{64,0},{1,65},{65,1},{2,66},{66,2},{3,67},{67,3},{4,68},{68... | collective-permute-start | bytes 1966088 | tf_op jit(solution)/shard_map/ppermute | solution.py:21
  195.4 50.0 %collective-permute-start.39 = (bf16[2,2,160,768]{3,2,1,0:T(8,128)(2,1)S(1)}, bf16[2,2,160,768]{3,2,1,0:T(8,128)(2,1)S(1)}, u32[]{:S(2)}, u32[]{:S(2)}) collective-permute-start(bf16[2,2,160,768]{3,2,1,0:T(8,128)(2,1)S(1)} %pad_maximum_fusion.refs_0_), channel_id=1, source_target_pairs={{0,16},{16,32},{32,48},{48,0},{1,17},{17,33},{33,49},{49,1},{2,18}... | collective-permute-start | bytes 2949128 | tf_op jit(solution)/shard_map/ppermute | solution.py:21
  196.2 49.5 %collective-permute-start.47 = (bf16[2,2,160,512]{3,2,1,0:T(8,128)(2,1)}, bf16[2,2,160,512]{3,2,1,0:T(8,128)(2,1)S(1)}, u32[]{:S(2)}, u32[]{:S(2)}) collective-permute-start(bf16[2,2,160,512]{3,2,1,0:T(8,128)(2,1)} %collective-permute-done.46.refs_15_), channel_id=1, source_target_pairs={{0,4},{4,8},{8,12},{12,0},{1,5},{5,9},{9,13},{13,1},{2,6},{6,10},{... | collective-permute-start | bytes 1966088 | tf_op jit(solution)/shard_map/ppermute | solution.py:21
  208.1 45.8 %collective-permute-start.45 = (bf16[2,2,160,512]{3,2,1,0:T(8,128)(2,1)}, bf16[2,2,160,512]{3,2,1,0:T(8,128)(2,1)S(1)}, u32[]{:S(2)}, u32[]{:S(2)}) collective-permute-start(bf16[2,2,160,512]{3,2,1,0:T(8,128)(2,1)} %collective-permute-done.43.refs_10_), channel_id=1, source_target_pairs={{0,12},{4,0},{8,4},{12,8},{1,13},{5,1},{9,5},{13,9},{2,14},{6,2},{... | collective-permute-start | bytes 1966088 | tf_op jit(solution)/shard_map/ppermute | solution.py:21
  223.2 31.7 %collective-permute-start.38 = (bf16[2,2,160,768]{3,2,1,0:T(8,128)(2,1)}, bf16[2,2,160,768]{3,2,1,0:T(8,128)(2,1)}, u32[]{:S(2)}, u32[]{:S(2)}) collective-permute-start(bf16[2,2,160,768]{3,2,1,0:T(8,128)(2,1)} %collective-permute-done.37.refs_7_), channel_id=1, source_target_pairs={{0,16},{16,32},{32,48},{48,0},{1,17},{17,33},{33,49},{49,1},{2,18}... | collective-permute-start | bytes 2949128 | tf_op jit(solution)/shard_map/ppermute | solution.py:21
  238.5 16.4 %collective-permute-start.36 = (bf16[2,2,160,768]{3,2,1,0:T(8,128)(2,1)}, bf16[2,2,160,768]{3,2,1,0:T(8,128)(2,1)}, u32[]{:S(2)}, u32[]{:S(2)}) collective-permute-start(bf16[2,2,160,768]{3,2,1,0:T(8,128)(2,1)} %collective-permute-done.34.refs_2_), channel_id=1, source_target_pairs={{0,48},{16,0},{32,16},{48,32},{1,49},{17,1},{33,17},{49,33},{2,50}... | collective-permute-start | bytes 2949128 | tf_op jit(solution)/shard_map/ppermute | solution.py:21
  238.5 5.9 %copy-start.23 = (f32[512,640]{1,0:T(8,128)S(1)}, f32[512,640]{1,0:T(8,128)}, u32[]{:S(2)}) copy-start(f32[512,640]{1,0:T(8,128)} %get-tuple-element.25) | copy-start | bytes 3932164
  245.7 8.3 %copy-start.21 = (bf16[2,2,160,768]{3,2,1,0:T(8,128)(2,1)}, bf16[2,2,160,768]{3,2,1,0:T(8,128)(2,1)S(1)}, u32[]{:S(2)}) copy-start(bf16[2,2,160,768]{3,2,1,0:T(8,128)(2,1)S(1)} %collective-permute-done.39.refs_6_) | copy-start | bytes 2949124
  245.7 11.0 %collective-permute-start.27 = (bf16[512,640]{1,0:T(8,128)(2,1)S(1)}, bf16[512,640]{1,0:T(8,128)(2,1)}, u32[]{:S(2)}, u32[]{:S(2)}) collective-permute-start(bf16[512,640]{1,0:T(8,128)(2,1)S(1)} %copy-done), channel_id=1, source_target_pairs={{0,2},{2,0},{1,3},{3,1},{4,6},{6,4},{5,7},{7,5},{8,10},{10,8},{9,1... | collective-permute-start | bytes 1966088 | tf_op jit(solution)/shard_map/ppermute | solution.py:21
  246.6 28.5 %collective-permute-start.26 = (bf16[512,640]{1,0:T(8,128)(2,1)}, bf16[512,640]{1,0:T(8,128)(2,1)}, u32[]{:S(2)}, u32[]{:S(2)}) collective-permute-start(bf16[512,640]{1,0:T(8,128)(2,1)} %add_convert_fusion.1), channel_id=1, source_target_pairs={{0,66},{64,0},{2,64},{66,2},{1,67},{65,1},{3,65},{67,3},{4,70},{68... | collective-permute-start | bytes 1966088 | tf_op jit(solution)/shard_map/ppermute | solution.py:26
  254.8 20.3 %collective-permute-start.28 = (bf16[512,640]{1,0:T(8,128)(2,1)}, bf16[512,640]{1,0:T(8,128)(2,1)}, u32[]{:S(2)}, u32[]{:S(2)}) collective-permute-start(bf16[512,640]{1,0:T(8,128)(2,1)} %add_convert_fusion.1), channel_id=1, source_target_pairs={{0,64},{64,2},{2,66},{66,0},{1,65},{65,3},{3,67},{67,1},{4,68},{68... | collective-permute-start | bytes 1966088 | tf_op jit(solution)/shard_map/ppermute | solution.py:26
  280.6 15.5 %copy-start.5 = (bf16[2,2,160,512]{3,2,1,0:T(8,128)(2,1)S(1)}, bf16[2,2,160,512]{3,2,1,0:T(8,128)(2,1)}, u32[]{:S(2)}) copy-start(bf16[2,2,160,512]{3,2,1,0:T(8,128)(2,1)} %copy-done.3) | copy-start | bytes 1966084
  280.6 15.5 %copy-start.8 = (bf16[2,2,160,512]{3,2,1,0:T(8,128)(2,1)S(1)}, bf16[2,2,160,512]{3,2,1,0:T(8,128)(2,1)}, u32[]{:S(2)}) copy-start(bf16[2,2,160,512]{3,2,1,0:T(8,128)(2,1)} %copy-done.6) | copy-start | bytes 1966084
  280.6 15.5 %copy-start.13 = (bf16[2,2,160,512]{3,2,1,0:T(8,128)(2,1)S(1)}, bf16[2,2,160,512]{3,2,1,0:T(8,128)(2,1)}, u32[]{:S(2)}) copy-start(bf16[2,2,160,512]{3,2,1,0:T(8,128)(2,1)} %copy-done.11) | copy-start | bytes 1966084
  289.6 16.3 %collective-permute-start.49 = (bf16[512,1280]{1,0:T(8,128)(2,1)}, bf16[512,1280]{1,0:T(8,128)(2,1)S(1)}, u32[]{:S(2)}, u32[]{:S(2)}) collective-permute-start(bf16[512,1280]{1,0:T(8,128)(2,1)} %project.2), channel_id=1, source_target_pairs={{0,1},{1,0},{2,3},{3,2},{4,5},{5,4},{6,7},{7,6},{8,9},{9,8},{10,11... | collective-permute-start | bytes 3932168 | tf_op jit(solution)/shard_map/ppermute | solution.py:21
  (17 other events, 28.1 us)
